TPU v7x, 32 devices: a whole 2x2x4 slice. The times are simulated.
32 devices in a mesh: blk: 16 (over z, x, core), sub: 2 (over y).
Axes of the slice: x: 2, y: 2, z: 4, core: 2. Of those that a mesh axis runs over, the one named last changes fastest.
Arguments:
- vectors: bfloat16 [16, 131072], P('sub', 'blk')
- energies: float32 [131072], P('blk'), may hold values from 1 to 4
- tile_values: bfloat16 [16, 128, 128, 128], P('blk', 'sub'), may hold values from -0.1875 to 0.1875
- tile_rows: int32 [16, 128], P('blk', 'sub'), may hold values from 0 to 63
- tile_cols: int32 [16, 128], P('blk', 'sub'), may hold values from 0 to 63
- tile_offsets: int32 [16, 128], P('blk', 'sub'), may hold values from 0 to 2, as said below
- tile_count: int32 [16, 2], P('blk', 'sub'), may hold values from 8 to 64, as said below
Outputs:
- residual: float32 [16, 131072], P('sub', 'blk')
Inputs may be any that keep to these rules, and one draw needn't show every extreme that they name: `tile_offsets`: an offset never exceeds the row block's index b; where the offset is 0, tile_rows >= tile_cols. `tile_count`: each count is 64 divided by 1, 2, 4 or 8.
All inputs are finite; a program needn't handle non-finite values.
Results may differ from a plain program's by a relative error of at most 0.0003.
Values may be sent and summed in bfloat16 or wider, within the bound.
No kernel may reach another device: no remote copies, remote signals or barrier semaphores. Data moves between devices by JAX's collectives and lax.ppermute only.
A program may use at most 64 MiB of HBM per device.

v0:
```python
import functools

import jax
import jax.numpy as jnp
from jax import lax
from jax.experimental import pallas as pl
from jax.experimental.pallas import tpu as pltpu
from jax.sharding import PartitionSpec as P

BW = 2
GROUP = 64
LIVE_UNIT = 65536
F32 = jnp.float32
BF16 = jnp.bfloat16
I32 = jnp.int32
ANY = pl.BlockSpec(memory_space=pl.ANY)
HBM = pl.BlockSpec(memory_space=pltpu.HBM)
VMEM = pl.BlockSpec(memory_space=pltpu.VMEM)
SMEM = pl.BlockSpec(memory_space=pltpu.SMEM)
NT = (((1,), (1,)), ((), ()))


def shifted(value, steps):
    count = lax.axis_size("blk")
    first, last = (max(0, -steps), min(count, count - steps))
    return lax.ppermute(value, "blk", [(source, source + steps) for source in range(first, last)])


def swap_sub(value):
    return lax.ppermute(value, "sub", [(0, 1), (1, 0)])


def swap_core(value):
    return lax.ppermute(value, "blk", [(i, i ^ 1) for i in range(lax.axis_size("blk"))])


def rounds_over(axis):
    count = lax.axis_size(axis)
    rounds, stride = [], 1
    while stride < count:
        rest = count // stride
        radix = next(p for p in range(2, rest + 1) if rest % p == 0)
        rounds.append((axis, stride, radix))
        stride *= radix
    return rounds


def run_rounds(value, rounds):
    for axis, stride, radix in rounds:
        total = value
        for turn in range(1, radix):
            pairs = []
            for source in range(lax.axis_size(axis)):
                digit = (source // stride) % radix
                pairs.append((source, source + ((digit + turn) % radix - digit) * stride))
            total = total + lax.ppermute(value, axis, pairs)
        value = total
    return value


def tile_at(index, side):
    return pl.ds(pl.multiple_of(index * side, side), side)


def split2(value):
    spread = value * 65537.0
    high = spread - (spread - value)
    return high, value - high


def odd_block():
    return lax.rem(lax.axis_index("blk"), 2) == 1


def in_order(own, other, out):
    rows = own.shape[0]
    first = lax.axis_index("sub") == 0

    @pl.when(first)
    def _():
        out[0:rows, :] = own[...]
        out[rows : 2 * rows, :] = other[...]

    @pl.when(jnp.logical_not(first))
    def _():
        out[0:rows, :] = other[...]
        out[rows : 2 * rows, :] = own[...]


def load_kernel(source, target, sem):
    copy = pltpu.make_async_copy(source, target, sem)
    copy.start()
    copy.wait()


def add_terms(table, slots, term_of, total, place, unrolled=False):
    count = table[0, 0] // LIVE_UNIT
    group_size = min(GROUP, slots)

    def add_group(group):
        first = group * group_size
        terms = [term_of(first + lane) for lane in range(group_size)]
        for lane, term in enumerate(terms):
            live = first + lane < count
            total[place(first + lane)] += jnp.where(live, term, 0.0)

    if unrolled and group_size == slots:
        add_group(0)
    else:
        pl.loop(0, pl.cdiv(count, group_size))(add_group)


def join_kernel(own, other, below, out):
    in_order(own, other, out)


def join_below_kernel(own, other, whole, term, out, across, later):
    in_order(own, other, out)
    later[...] = term[...]
    odd = odd_block()

    @pl.when(odd)
    def _():
        across[...] = out[...]

    @pl.when(jnp.logical_not(odd))
    def _():
        across[...] = whole[...]


def levels_at(energies, start, step):
    side = energies.shape[1]
    rows = [energies[pl.ds((start + i) // side, 1), :] for i in range(0, step, side)]
    return jnp.concatenate(rows, 1)


def mirror_kernel(table, vec, energies, tiles, m0, m1, m2, small, acc):
    side = tiles.shape[-1]
    width, rows_dev = vec.shape
    acc[...] = jnp.zeros_like(acc)

    add_terms(
        table,
        tiles.shape[0],
        lambda slot: jnp.dot(
            vec[:, tile_at(table[0, slot] % LIVE_UNIT, side)], tiles[slot], preferred_element_type=F32
        ),
        acc,
        lambda slot: (table[2, slot], slice(None), tile_at(table[1, slot], side)),
        unrolled=True,
    )
    m0[...] = acc[0]
    m1[...] = acc[1]
    m2[...] = acc[2]
    total = jnp.zeros((width, 3 * width), F32)
    step = 2 * side
    for start in range(0, rows_dev, step):
        v = vec[:, pl.ds(start, step)]
        scaled = split2(levels_at(energies, start, step) * v.astype(F32))
        total += lax.dot_general(
            v,
            jnp.concatenate([v] + [part.astype(BF16) for part in scaled], 0),
            NT,
            preferred_element_type=F32,
        )
    total *= 1.0 / lax.axis_size("sub")
    small[0:width, 0:width] = total[:, :width]
    small[width : 2 * width, 0:width] = total[:, width : 2 * width] + total[:, 2 * width :]


def write_parts(columns, value, targets):
    if len(targets) == 1:
        targets[0][...] = value(slice(None))
        return
    mine = lax.axis_index("sub") * columns
    for start, target in zip((mine, columns - mine), targets):
        target[...] = value(pl.ds(pl.multiple_of(start, columns), columns))


def up_kernel(columns, m2, crossed, ready, *targets):
    odd = odd_block()

    @pl.when(odd)
    def _():
        write_parts(columns, lambda rows: m2[rows, :] + crossed[rows, :], targets)

    @pl.when(jnp.logical_not(odd))
    def _():
        write_parts(columns, lambda rows: m2[rows, :], targets)


def sum_kernel(first, second, ready, out):
    out[...] = first[...] + second[...]


def direct_kernel(
    columns, table, vec, vec1, vec2, tiles, m0, crossed, before, *rest
):
    targets, (small, sources, own) = rest[:-3], rest[-3:]
    side = tiles.shape[-1]
    width, rows_dev = vec.shape
    own[...] = jnp.zeros_like(own)
    sources[0] = vec[...]
    sources[1] = vec1[...]
    sources[2] = vec2[...]

    add_terms(
        table,
        tiles.shape[0],
        lambda slot: lax.dot_general(
            sources[table[2, slot], :, tile_at(table[1, slot], side)],
            tiles[slot],
            NT,
            preferred_element_type=F32,
        ),
        own,
        lambda slot: (slice(None), tile_at(table[0, slot] % LIVE_UNIT, side)),
    )
    left = jnp.zeros((width, 2 * width), F32)
    step = 2 * side
    for start in range(0, rows_dev, step):
        here = pl.ds(start, step)
        v = vec[:, here]
        parts = jnp.concatenate([part.astype(BF16) for part in split2(own[:, here])], 0)
        left += lax.dot_general(v, parts, NT, preferred_element_type=F32)
    cross = left[:, :width] + left[:, width:]
    small[0:width, 0:width] = before[0:width, 0:width]
    small[width : 2 * width, 0:width] = before[width : 2 * width, 0:width] + (
        cross + cross.T
    )
    odd = odd_block()

    @pl.when(odd)
    def _():
        write_parts(columns, lambda part: own[part, :] + m0[part, :], targets)

    @pl.when(jnp.logical_not(odd))
    def _():
        write_parts(
            columns, lambda part: own[part, :] + (m0[part, :] + crossed[part, :]), targets
        )


def eliminate(system):
    width = system.shape[1]
    col_id = lax.broadcasted_iota(I32, system.shape, 1)
    for pivot in range(0, width, 2):
        col0, col1 = [
            jnp.broadcast_to(system[:, i : i + 1], system.shape) for i in (pivot, pivot + 1)
        ]
        row0, row1 = [
            jnp.broadcast_to(system[i : i + 1, :], system.shape) for i in (pivot, pivot + 1)
        ]
        a, c, b, d = [
            jnp.broadcast_to(col[i : i + 1, :], system.shape)
            for col in (col0, col1)
            for i in (pivot, pivot + 1)
        ]
        ratio = b / a
        new1 = (col1 - col0 * ratio) / (d - c * ratio)
        new0 = col0 / a - new1 * (c / a)
        system = system - (new0 * row0 + new1 * row1)
        system = jnp.where(col_id == pivot, new0, jnp.where(col_id == pivot + 1, new1, system))
    return system[width:, :]


def model_kernel(small, vec, mine, energies, *rest):
    terms, (out, coeffs) = rest[:-2], rest[-2:]
    width, rows_dev = vec.shape
    columns = mine.shape[0]
    side = energies.shape[1]
    coeffs[...] = eliminate(small[:, :width])
    wanted = coeffs[pl.ds(lax.axis_index("sub") * columns, columns), :]
    high, rest_of = split2(wanted)
    mid, low = split2(rest_of)
    factors = jnp.concatenate([high, mid, low], 0).astype(BF16)
    step = 8 * side
    for start in range(0, rows_dev, step):
        here = pl.ds(start, step)
        model = jnp.dot(factors, vec[:, here], preferred_element_type=F32)
        model = model[:columns] + (model[columns : 2 * columns] + model[2 * columns :])
        applied = levels_at(energies, start, step) * mine[:, here].astype(F32)
        for term in terms:
            applied = applied + term[:, here]
        out[:, here] = applied - model


def last_kernel(first, second, out):
    out[...] = first[...] + second[...]


def call(kernel, name, out_shape, in_specs, out_specs, args, cycles, scratch=(), room=24):
    return pl.pallas_call(
        kernel,
        out_shape=out_shape,
        in_specs=in_specs,
        out_specs=out_specs,
        scratch_shapes=list(scratch),
        compiler_params=pltpu.CompilerParams(vmem_limit_bytes=room * 1024 * 1024),
        cost_estimate=pl.CostEstimate(
            flops=0, bytes_accessed=cycles * 3_000_000, transcendentals=0
        ),
        name=name,
    )(*args)


def on_device(vectors, energies, tile_values, tile_rows, tile_cols, tile_offsets, tile_count):
    columns, rows_dev = vectors.shape
    n_sub = lax.axis_size("sub")
    pair = n_sub == 2
    width = columns * n_sub
    slots, side = tile_values.shape[1:3]
    levels = energies.reshape(rows_dev // side, side)
    narrow = jax.ShapeDtypeStruct((width, rows_dev), BF16)
    block = jax.ShapeDtypeStruct((width, rows_dev), F32)
    half = jax.ShapeDtypeStruct((columns, rows_dev), F32)
    square = jax.ShapeDtypeStruct((2 * width, side), F32)
    parts = [half] * 2 if pair else [block]

    table = jnp.concatenate(
        [tile_rows + LIVE_UNIT * tile_count, tile_cols, tile_offsets], 0
    )
    tiles = call(
        load_kernel,
        "load",
        jax.ShapeDtypeStruct((slots, side, side), BF16),
        [HBM],
        VMEM,
        (tile_values.reshape(slots, side, side),),
        1,
        [pltpu.SemaphoreType.DMA],
        51,
    )
    if pair:
        other = swap_sub(vectors)
        below = shifted(vectors, BW)
        whole = call(join_kernel, "join", narrow, [VMEM] * 3, VMEM, (vectors, other, below), 1)
    else:
        whole = lax.all_gather(vectors, "sub", axis=0, tiled=True)
    m0, m1, m2, before = call(
        mirror_kernel,
        "mirror",
        [block] * 3 + [square],
        [SMEM] + [VMEM] * 3,
        [VMEM] * 4,
        (table, whole, levels, tiles),
        2,
        [pltpu.VMEM((BW + 1, width, rows_dev), F32)],
    )
    if pair:
        whole2, across, m1 = call(
            join_below_kernel,
            "join_below",
            [narrow] * 2 + [block],
            [VMEM] * 4,
            [VMEM] * 3,
            (below, swap_sub(below), whole, m1),
            1,
        )
    else:
        whole2 = shifted(whole, BW)
        across = jnp.where(lax.rem(lax.axis_index("blk"), 2) == 1, whole2, whole)
    whole1 = swap_core(across)
    crossed = swap_core(m1)
    up = call(
        functools.partial(up_kernel, columns),
        "up",
        parts,
        [VMEM] * 2 + [ANY],
        [VMEM] * len(parts),
        (m2, crossed, m2),
        1,
    )
    *own, small = call(
        functools.partial(direct_kernel, columns),
        "direct",
        parts + [square],
        [SMEM] + [VMEM] * 7,
        [VMEM] * (len(parts) + 1),
        (table, whole, whole1, whole2, tiles, m0, crossed, before),
        3,
        [pltpu.VMEM((BW + 1, width, rows_dev), BF16), pltpu.VMEM((width, rows_dev), F32)],
    )
    first, *others = rounds_over("blk")
    rounds = others + [first] + rounds_over("sub")
    stages = [small]
    for one in rounds:
        stages.append(run_rounds(stages[-1], [one]))
    small = stages[-1]
    if pair:
        up = call(
            sum_kernel,
            "sum",
            half,
            [VMEM] * 2 + [ANY],
            VMEM,
            (up[0], swap_sub(up[1]), stages[len(others)]),
            1,
        )
        terms = [own[0], swap_sub(own[1])]
    else:
        up = lax.psum_scatter(up[0], "sub", scatter_dimension=0, tiled=True)
        terms = [lax.psum_scatter(own[0], "sub", scatter_dimension=0, tiled=True)]
    nearly = call(
        model_kernel,
        "model",
        half,
        [VMEM] * (4 + len(terms)),
        VMEM,
        (small, whole, vectors, levels, *terms),
        2,
        [pltpu.VMEM((width, width), F32)],
    )
    return call(last_kernel, "last", half, [VMEM] * 2, VMEM, (nearly, shifted(up, -BW)), 1)


def solution(mesh):
    in_specs = (
        P("sub", "blk"),
        P("blk"),
        P("blk", "sub", None, None),
        P("blk", "sub"),
        P("blk", "sub"),
        P("blk", "sub"),
        P("blk", "sub"),
    )
    out_specs = P("sub", "blk")
    return jax.shard_map(
        on_device, mesh=mesh, in_specs=in_specs, out_specs=out_specs, check_vma=False
    )
```

profile of v0, /device:TPU:0, one launch (start us, length us, event | category | flops | bytes accessed | tf_op | source)
XLA Modules:
  0.0 41.6 jit_solution(18053110996979240294)
XLA Ops:
  0.0 4.8 %collective-permute-start.1 = (bf16[8,8192]{1,0:T(8,128)(2,1)}, bf16[8,8192]{1,0:T(8,128)(2,1)S(1)}, u32[]{:S(2)}, u32[]{:S(2)}) collective-permute-start(bf16[8,8192]{1,0:T(8,128)(2,1)} %mine.1), channel_id=1, source_target_pairs={{0,4},{2,6},{4,8},{6,10},{8,12},{10,14},{12,16},{14,18},{16,20},{1... | collective-permute-start | bytes 393224 | tf_op jit(solution)/shard_map/ppermute | solution.py:26
  4.8 1.6 %collective-permute-start = (bf16[8,8192]{1,0:T(8,128)(2,1)}, bf16[8,8192]{1,0:T(8,128)(2,1)S(1)}, u32[]{:S(2)}, u32[]{:S(2)}) collective-permute-start(bf16[8,8192]{1,0:T(8,128)(2,1)} %mine.1), channel_id=1, source_target_pairs={{0,1},{1,0},{2,3},{3,2},{4,5},{5,4},{6,7},{7,6},{8,9},{9,8},{10,11... | collective-permute-start | bytes 393224 | tf_op jit(solution)/shard_map/ppermute | solution.py:30
  7.1 0.8 %collective-permute-done.1.below.own = bf16[8,8192]{1,0:T(8,128)(2,1)S(1)} collective-permute-done((bf16[8,8192]{1,0:T(8,128)(2,1)}, bf16[8,8192]{1,0:T(8,128)(2,1)S(1)}, u32[]{:S(2)}, u32[]{:S(2)}) %collective-permute-start.1) | collective-permute-done | bytes 131104 | tf_op jit(solution)/shard_map/ppermute | solution.py:26
  7.9 1.5 %collective-permute-start.2 = (bf16[8,8192]{1,0:T(8,128)(2,1)S(1)}, bf16[8,8192]{1,0:T(8,128)(2,1)S(1)}, u32[]{:S(2)}, u32[]{:S(2)}) collective-permute-start(bf16[8,8192]{1,0:T(8,128)(2,1)S(1)} %collective-permute-done.1.below.own), channel_id=1, source_target_pairs={{0,1},{1,0},{2,3},{3,2},{4,5},{5,4},{6,7},{7,6},{8,9},{9,8},{10,11... | collective-permute-start | bytes 393224 | tf_op jit(solution)/shard_map/ppermute | solution.py:30
  9.4 0.7 %broadcast_add_fusion = s32[1,64]{1,0:T(1,128)S(1)} fusion(s32[1,64]{1,0:T(1,128)} %param.10, s32[]{:T(128)} %bitcast), kind=kLoop, calls=%fused_computation.1 | loop fusion | flops 64 | bytes 516 | tf_op jit(solution)/shard_map/add | solution.py:321
  10.1 1.6 %load.1.tiles = bf16[64,128,128]{2,1,0:T(8,128)(2,1)S(1)} custom-call(bf16[64,128,128]{2,1,0:T(8,128)(2,1)} %bitcast.5), custom_call_target="tpu_custom_call" | custom-call | bytes 3000000 | tf_op jit(solution)/shard_map/load/pallas_call | solution.py:293
  11.8 1.7 %mirror.1 = (f32[16,8192]{1,0:T(8,128)S(1)}, f32[16,8192]{1,0:T(8,128)S(1)}, f32[16,8192]{1,0:T(8,128)S(1)}, f32[32,128]{1,0:T(8,128)S(1)}) custom-call(s32[3,64]{1,0:T(4,128)S(1)} %pad_add_fusion.table, bf16[16,8192]{1,0:T(8,128)(2,1)S(1)} %join.1.vec.whole, f32[64,128]{1,0:T(8,128)S(1)} %bitcast.3, bf16[64,128,128]{2,1,0:T(8,128)(2,1)S(1)} %load.1.tiles), custom_call_target="tpu_custom_call" | custom-call | bytes 6000000 | tf_op jit(solution)/shard_map/mirror/pallas_call | solution.py:293
  14.2 1.4 %collective-permute-done.4.crossed = f32[16,8192]{1,0:T(8,128)S(1)} collective-permute-done((f32[16,8192]{1,0:T(8,128)S(1)}, f32[16,8192]{1,0:T(8,128)S(1)}, u32[]{:S(2)}, u32[]{:S(2)}) %collective-permute-start.4) | collective-permute-done | bytes 524320 | tf_op jit(solution)/shard_map/ppermute | solution.py:34
  15.6 1.0 %collective-permute-start.11 = (f32[8,8192]{1,0:T(8,128)S(1)}, f32[8,8192]{1,0:T(8,128)S(1)}, u32[]{:S(2)}, u32[]{:S(2)}) collective-permute-start(f32[8,8192]{1,0:T(8,128)S(1)} %get-tuple-element.28), channel_id=1, source_target_pairs={{0,1},{1,0},{2,3},{3,2},{4,5},{5,4},{6,7},{7,6},{8,9},{9,8},{10,11... | collective-permute-start | bytes 786440 | tf_op jit(solution)/shard_map/ppermute | solution.py:30
  16.6 2.4 %direct.1 = (f32[8,8192]{1,0:T(8,128)S(1)}, f32[8,8192]{1,0:T(8,128)S(1)}, f32[32,128]{1,0:T(8,128)S(1)}) custom-call(s32[3,64]{1,0:T(4,128)S(1)} %pad_add_fusion.table, bf16[16,8192]{1,0:T(8,128)(2,1)S(1)} %join.1.vec.whole, bf16[16,8192]{1,0:T(8,128)(2,1)S(1)} %collective-permute-done.3.vec1, bf16[16,8192]{1,0:T(8,128)(2,1)S(1)} %get-tuple-element.19.vec2, ...), custom_call_target="tpu_custom_call" | custom-call | bytes 9000000 | tf_op jit(solution)/shard_map/direct/pallas_call | solution.py:293
  19.0 2.4 %collective-permute-start.5 = (f32[32,128]{1,0:T(8,128)S(1)}, f32[32,128]{1,0:T(8,128)S(1)}, u32[]{:S(2)}, u32[]{:S(2)}) collective-permute-start(f32[32,128]{1,0:T(8,128)S(1)} %get-tuple-element.23), channel_id=1, source_target_pairs={{0,4},{2,6},{4,0},{6,2},{8,12},{10,14},{12,8},{14,10},{16,20},{18,... | collective-permute-start | bytes 49160 | tf_op jit(solution)/shard_map/ppermute | solution.py:56
  21.4 1.7 %collective-permute-done.5 = f32[32,128]{1,0:T(8,128)S(1)} collective-permute-done((f32[32,128]{1,0:T(8,128)S(1)}, f32[32,128]{1,0:T(8,128)S(1)}, u32[]{:S(2)}, u32[]{:S(2)}) %collective-permute-start.5) | collective-permute-done | bytes 16416 | tf_op jit(solution)/shard_map/ppermute | solution.py:56
  23.1 3.0 %collective-permute-start.6 = (f32[32,128]{1,0:T(8,128)S(1)}, f32[32,128]{1,0:T(8,128)S(1)}, u32[]{:S(2)}, u32[]{:S(2)}) collective-permute-start(f32[32,128]{1,0:T(8,128)S(1)} %add.28), channel_id=1, source_target_pairs={{0,8},{2,10},{4,12},{6,14},{8,0},{10,2},{12,4},{14,6},{16,24},{18,... | collective-permute-start | bytes 49160 | tf_op jit(solution)/shard_map/ppermute | solution.py:56
  26.1 1.7 %collective-permute-done.6 = f32[32,128]{1,0:T(8,128)S(1)} collective-permute-done((f32[32,128]{1,0:T(8,128)S(1)}, f32[32,128]{1,0:T(8,128)S(1)}, u32[]{:S(2)}, u32[]{:S(2)}) %collective-permute-start.6) | collective-permute-done | bytes 16416 | tf_op jit(solution)/shard_map/ppermute | solution.py:56
  27.8 3.0 %collective-permute-start.7 = (f32[32,128]{1,0:T(8,128)S(1)}, f32[32,128]{1,0:T(8,128)S(1)}, u32[]{:S(2)}, u32[]{:S(2)}) collective-permute-start(f32[32,128]{1,0:T(8,128)S(1)} %add.29), channel_id=1, source_target_pairs={{0,16},{2,18},{4,20},{6,22},{8,24},{10,26},{12,28},{14,30},{16,0},... | collective-permute-start | bytes 49160 | tf_op jit(solution)/shard_map/ppermute | solution.py:56
  30.8 1.2 %collective-permute-start.10 = (f32[8,8192]{1,0:T(8,128)S(1)}, f32[8,8192]{1,0:T(8,128)S(1)}, u32[]{:S(2)}, u32[]{:S(2)}) collective-permute-start(f32[8,8192]{1,0:T(8,128)S(1)} %get-tuple-element.25), channel_id=1, source_target_pairs={{0,1},{1,0},{2,3},{3,2},{4,5},{5,4},{6,7},{7,6},{8,9},{9,8},{10,11... | collective-permute-start | bytes 786440 | tf_op jit(solution)/shard_map/ppermute | solution.py:30
  32.0 0.5 %collective-permute-done.7 = f32[32,128]{1,0:T(8,128)S(1)} collective-permute-done((f32[32,128]{1,0:T(8,128)S(1)}, f32[32,128]{1,0:T(8,128)S(1)}, u32[]{:S(2)}, u32[]{:S(2)}) %collective-permute-start.7) | collective-permute-done | bytes 16416 | tf_op jit(solution)/shard_map/ppermute | solution.py:56
  32.6 1.3 %collective-permute-start.12 = (f32[8,8192]{1,0:T(8,128)S(1)}, f32[8,8192]{1,0:T(8,128)S(1)}, u32[]{:S(2)}, u32[]{:S(2)}) collective-permute-start(f32[8,8192]{1,0:T(8,128)S(1)} %sum.1), channel_id=1, source_target_pairs={{4,0},{6,2},{8,4},{10,6},{12,8},{14,10},{16,12},{18,14},{20,16},{2... | collective-permute-start | bytes 786440 | tf_op jit(solution)/shard_map/ppermute | solution.py:26
  34.0 1.2 %collective-permute-done.8 = f32[32,128]{1,0:T(8,128)S(1)} collective-permute-done((f32[32,128]{1,0:T(8,128)S(1)}, f32[32,128]{1,0:T(8,128)S(1)}, u32[]{:S(2)}, u32[]{:S(2)}) %collective-permute-start.8) | collective-permute-done | bytes 16416 | tf_op jit(solution)/shard_map/ppermute | solution.py:56
  35.2 1.2 %collective-permute-start.9 = (f32[32,128]{1,0:T(8,128)S(1)}, f32[32,128]{1,0:T(8,128)S(1)}, u32[]{:S(2)}, u32[]{:S(2)}) collective-permute-start(f32[32,128]{1,0:T(8,128)S(1)} %add.31), channel_id=1, source_target_pairs={{0,1},{1,0},{2,3},{3,2},{4,5},{5,4},{6,7},{7,6},{8,9},{9,8},{10,11... | collective-permute-start | bytes 49160 | tf_op jit(solution)/shard_map/ppermute | solution.py:56
  36.3 2.6 %collective-permute-done.9 = f32[32,128]{1,0:T(8,128)S(1)} collective-permute-done((f32[32,128]{1,0:T(8,128)S(1)}, f32[32,128]{1,0:T(8,128)S(1)}, u32[]{:S(2)}, u32[]{:S(2)}) %collective-permute-start.9) | collective-permute-done | bytes 16416 | tf_op jit(solution)/shard_map/ppermute | solution.py:56
  38.9 1.3 %model.1.first = f32[8,8192]{1,0:T(8,128)S(1)} custom-call(f32[32,128]{1,0:T(8,128)S(1)} %add.32.small, bf16[16,8192]{1,0:T(8,128)(2,1)S(1)} %join.1.vec.whole, bf16[8,8192]{1,0:T(8,128)(2,1)S(1)} %copy-done, f32[64,128]{1,0:T(8,128)S(1)} %bitcast.4, f32[8,8192]{1,0:T(8,128)S(1)} %get-tuple-element.24.rest_0_, f32[8,8192]{1,0:T(8,128)S(1)} %collective-permute-done.10.rest_1_), custom_call_target="tpu_custom_call" | custom-call | bytes 6000000 | tf_op jit(solution)/shard_map/model/pallas_call | solution.py:293
  40.2 0.6 %collective-permute-done.12.second = f32[8,8192]{1,0:T(8,128)S(1)} collective-permute-done((f32[8,8192]{1,0:T(8,128)S(1)}, f32[8,8192]{1,0:T(8,128)S(1)}, u32[]{:S(2)}, u32[]{:S(2)}) %collective-permute-start.12) | collective-permute-done | bytes 262176 | tf_op jit(solution)/shard_map/ppermute | solution.py:26
  40.9 0.7 %last.1 = f32[8,8192]{1,0:T(8,128)} custom-call(f32[8,8192]{1,0:T(8,128)S(1)} %model.1.first, f32[8,8192]{1,0:T(8,128)S(1)} %collective-permute-done.12.second), custom_call_target="tpu_custom_call" | custom-call | bytes 3000000 | tf_op jit(solution)/shard_map/last/pallas_call | solution.py:293
  (26 shorter events, 0.9 us)
Async XLA Ops:
  0.0 7.9 %collective-permute-start.1 = (bf16[8,8192]{1,0:T(8,128)(2,1)}, bf16[8,8192]{1,0:T(8,128)(2,1)S(1)}, u32[]{:S(2)}, u32[]{:S(2)}) collective-permute-start(bf16[8,8192]{1,0:T(8,128)(2,1)} %mine.1), channel_id=1, source_target_pairs={{0,4},{2,6},{4,8},{6,10},{8,12},{10,14},{12,16},{14,18},{16,20},{1... | collective-permute-start | bytes 393224 | tf_op jit(solution)/shard_map/ppermute | solution.py:26
  4.8 6.9 %collective-permute-start = (bf16[8,8192]{1,0:T(8,128)(2,1)}, bf16[8,8192]{1,0:T(8,128)(2,1)S(1)}, u32[]{:S(2)}, u32[]{:S(2)}) collective-permute-start(bf16[8,8192]{1,0:T(8,128)(2,1)} %mine.1), channel_id=1, source_target_pairs={{0,1},{1,0},{2,3},{3,2},{4,5},{5,4},{6,7},{7,6},{8,9},{9,8},{10,11... | collective-permute-start | bytes 393224 | tf_op jit(solution)/shard_map/ppermute | solution.py:30
  7.9 5.6 %collective-permute-start.2 = (bf16[8,8192]{1,0:T(8,128)(2,1)S(1)}, bf16[8,8192]{1,0:T(8,128)(2,1)S(1)}, u32[]{:S(2)}, u32[]{:S(2)}) collective-permute-start(bf16[8,8192]{1,0:T(8,128)(2,1)S(1)} %collective-permute-done.1.below.own), channel_id=1, source_target_pairs={{0,1},{1,0},{2,3},{3,2},{4,5},{5,4},{6,7},{7,6},{8,9},{9,8},{10,11... | collective-permute-start | bytes 393224 | tf_op jit(solution)/shard_map/ppermute | solution.py:30
  10.1 1.7 %copy-start.2 = (s32[1,64]{1,0:T(1,128)S(1)}, s32[1,64]{1,0:T(1,128)}, u32[]{:S(2)}) copy-start(s32[1,64]{1,0:T(1,128)} %param.12) | copy-start | bytes 772
  10.1 1.7 %copy-start.3 = (s32[1,64]{1,0:T(1,128)S(1)}, s32[1,64]{1,0:T(1,128)}, u32[]{:S(2)}) copy-start(s32[1,64]{1,0:T(1,128)} %param.11) | copy-start | bytes 772
  10.1 1.7 %copy-start = (bf16[8,8192]{1,0:T(8,128)(2,1)S(1)}, bf16[8,8192]{1,0:T(8,128)(2,1)}, u32[]{:S(2)}) copy-start(bf16[8,8192]{1,0:T(8,128)(2,1)} %mine.1) | copy-start | bytes 393220
  10.1 1.8 %copy-start.1 = (f32[8192]{0:T(1024)S(1)}, f32[8192]{0:T(1024)}, u32[]{:S(2)}) copy-start(f32[8192]{0:T(1024)} %param.8) | copy-start | bytes 98308
  13.6 2.0 %collective-permute-start.4 = (f32[16,8192]{1,0:T(8,128)S(1)}, f32[16,8192]{1,0:T(8,128)S(1)}, u32[]{:S(2)}, u32[]{:S(2)}) collective-permute-start(f32[16,8192]{1,0:T(8,128)S(1)} %get-tuple-element.21), channel_id=1, source_target_pairs={{0,2},{2,0},{4,6},{6,4},{8,10},{10,8},{12,14},{14,12},{16,18},{18,... | collective-permute-start | bytes 1572872 | tf_op jit(solution)/shard_map/ppermute | solution.py:34
  13.7 2.9 %collective-permute-start.3 = (bf16[16,8192]{1,0:T(8,128)(2,1)S(1)}, bf16[16,8192]{1,0:T(8,128)(2,1)S(1)}, u32[]{:S(2)}, u32[]{:S(2)}) collective-permute-start(bf16[16,8192]{1,0:T(8,128)(2,1)S(1)} %get-tuple-element.18), channel_id=1, source_target_pairs={{0,2},{2,0},{4,6},{6,4},{8,10},{10,8},{12,14},{14,12},{16,18},{18,... | collective-permute-start | bytes 786440 | tf_op jit(solution)/shard_map/ppermute | solution.py:34
  15.6 16.9 %collective-permute-start.11 = (f32[8,8192]{1,0:T(8,128)S(1)}, f32[8,8192]{1,0:T(8,128)S(1)}, u32[]{:S(2)}, u32[]{:S(2)}) collective-permute-start(f32[8,8192]{1,0:T(8,128)S(1)} %get-tuple-element.28), channel_id=1, source_target_pairs={{0,1},{1,0},{2,3},{3,2},{4,5},{5,4},{6,7},{7,6},{8,9},{9,8},{10,11... | collective-permute-start | bytes 786440 | tf_op jit(solution)/shard_map/ppermute | solution.py:30
  19.0 4.1 %collective-permute-start.5 = (f32[32,128]{1,0:T(8,128)S(1)}, f32[32,128]{1,0:T(8,128)S(1)}, u32[]{:S(2)}, u32[]{:S(2)}) collective-permute-start(f32[32,128]{1,0:T(8,128)S(1)} %get-tuple-element.23), channel_id=1, source_target_pairs={{0,4},{2,6},{4,0},{6,2},{8,12},{10,14},{12,8},{14,10},{16,20},{18,... | collective-permute-start | bytes 49160 | tf_op jit(solution)/shard_map/ppermute | solution.py:56
  23.1 4.7 %collective-permute-start.6 = (f32[32,128]{1,0:T(8,128)S(1)}, f32[32,128]{1,0:T(8,128)S(1)}, u32[]{:S(2)}, u32[]{:S(2)}) collective-permute-start(f32[32,128]{1,0:T(8,128)S(1)} %add.28), channel_id=1, source_target_pairs={{0,8},{2,10},{4,12},{6,14},{8,0},{10,2},{12,4},{14,6},{16,24},{18,... | collective-permute-start | bytes 49160 | tf_op jit(solution)/shard_map/ppermute | solution.py:56
  27.8 4.8 %collective-permute-start.7 = (f32[32,128]{1,0:T(8,128)S(1)}, f32[32,128]{1,0:T(8,128)S(1)}, u32[]{:S(2)}, u32[]{:S(2)}) collective-permute-start(f32[32,128]{1,0:T(8,128)S(1)} %add.29), channel_id=1, source_target_pairs={{0,16},{2,18},{4,20},{6,22},{8,24},{10,26},{12,28},{14,30},{16,0},... | collective-permute-start | bytes 49160 | tf_op jit(solution)/shard_map/ppermute | solution.py:56
  30.8 8.1 %collective-permute-start.10 = (f32[8,8192]{1,0:T(8,128)S(1)}, f32[8,8192]{1,0:T(8,128)S(1)}, u32[]{:S(2)}, u32[]{:S(2)}) collective-permute-start(f32[8,8192]{1,0:T(8,128)S(1)} %get-tuple-element.25), channel_id=1, source_target_pairs={{0,1},{1,0},{2,3},{3,2},{4,5},{5,4},{6,7},{7,6},{8,9},{9,8},{10,11... | collective-permute-start | bytes 786440 | tf_op jit(solution)/shard_map/ppermute | solution.py:30
  32.6 8.3 %collective-permute-start.12 = (f32[8,8192]{1,0:T(8,128)S(1)}, f32[8,8192]{1,0:T(8,128)S(1)}, u32[]{:S(2)}, u32[]{:S(2)}) collective-permute-start(f32[8,8192]{1,0:T(8,128)S(1)} %sum.1), channel_id=1, source_target_pairs={{4,0},{6,2},{8,4},{10,6},{12,8},{14,10},{16,12},{18,14},{20,16},{2... | collective-permute-start | bytes 786440 | tf_op jit(solution)/shard_map/ppermute | solution.py:26
  33.9 1.2 %collective-permute-start.8 = (f32[32,128]{1,0:T(8,128)S(1)}, f32[32,128]{1,0:T(8,128)S(1)}, u32[]{:S(2)}, u32[]{:S(2)}) collective-permute-start(f32[32,128]{1,0:T(8,128)S(1)} %add.30.ready), channel_id=1, source_target_pairs={{0,2},{2,0},{4,6},{6,4},{8,10},{10,8},{12,14},{14,12},{16,18},{18,... | collective-permute-start | bytes 49160 | tf_op jit(solution)/shard_map/ppermute | solution.py:56
  35.2 3.7 %collective-permute-start.9 = (f32[32,128]{1,0:T(8,128)S(1)}, f32[32,128]{1,0:T(8,128)S(1)}, u32[]{:S(2)}, u32[]{:S(2)}) collective-permute-start(f32[32,128]{1,0:T(8,128)S(1)} %add.31), channel_id=1, source_target_pairs={{0,1},{1,0},{2,3},{3,2},{4,5},{5,4},{6,7},{7,6},{8,9},{9,8},{10,11... | collective-permute-start | bytes 49160 | tf_op jit(solution)/shard_map/ppermute | solution.py:56
where the time goes:
time: 41.8 us; the launch traced here: 41.6 us
  starting transfers between devices  21.6 us (52%)
  waiting for transfers between devices  10.5 us (25%)
  Pallas kernels  7.92 us (19%)
  between operations  0.81 us (2%)
  other arithmetic  0.69 us (2%)
    ppermute x5, starting transfers between devices, run_rounds(): total = total + lax.ppermute(value, axis, pairs)  9.68 us
    pallas_call x9, Pallas kernels, call(): pl.pallas_call(kernel, out_shape=out_shape, in_specs=in_specs, out_specs=...  7.92 us
    ppermute x5, waiting for transfers between devices, run_rounds(): total = total + lax.ppermute(value, axis, pairs)  7.71 us
    ppermute x2, starting transfers between devices, shifted(): lax.ppermute(value, 'blk', [(source, source + steps) for source in range(...  6.13 us
    ppermute x4, starting transfers between devices, swap_sub(): return lax.ppermute(value, 'sub', [(0, 1), (1, 0)])  5.23 us
    ppermute x2, waiting for transfers between devices, shifted(): lax.ppermute(value, 'blk', [(source, source + steps) for source in range(...  1.43 us
    ppermute x2, waiting for transfers between devices, swap_core(): lax.ppermute(value, 'blk', [(i, i ^ 1) for i in range(lax.axis_size('blk'...  1.4 us
  transfers between devices with their start and end apart: 13, of which 8 were waited for; matrix products, arithmetic and copies ran while one was open for 2% of the time, Pallas kernels for 17%

commit v1 on v0

--- a/solution.py
+++ b/solution.py
@@ -110,13 +110,12 @@
         pl.loop(0, pl.cdiv(count, group_size))(add_group)
 
 
-def join_kernel(own, other, below, out):
+def join_kernel(own, other, out):
     in_order(own, other, out)
 
 
-def join_below_kernel(own, other, whole, term, out, across, later):
+def join_below_kernel(own, other, whole, out, across):
     in_order(own, other, out)
-    later[...] = term[...]
     odd = odd_block()
 
     @pl.when(odd)
@@ -289,7 +288,7 @@
     out[...] = first[...] + second[...]
 
 
-def call(kernel, name, out_shape, in_specs, out_specs, args, cycles, scratch=(), room=24):
+def call(kernel, name, out_shape, in_specs, out_specs, args, cycles, scratch=(), room=24, flops=0):
     return pl.pallas_call(
         kernel,
         out_shape=out_shape,
@@ -298,7 +297,7 @@
         scratch_shapes=list(scratch),
         compiler_params=pltpu.CompilerParams(vmem_limit_bytes=room * 1024 * 1024),
         cost_estimate=pl.CostEstimate(
-            flops=0, bytes_accessed=cycles * 3_000_000, transcendentals=0
+            flops=flops, bytes_accessed=cycles * 3_000_000, transcendentals=0
         ),
         name=name,
     )(*args)
@@ -330,11 +329,12 @@
         1,
         [pltpu.SemaphoreType.DMA],
         51,
+        20_000_000_000,
     )
     if pair:
         other = swap_sub(vectors)
         below = shifted(vectors, BW)
-        whole = call(join_kernel, "join", narrow, [VMEM] * 3, VMEM, (vectors, other, below), 1)
+        whole = call(join_kernel, "join", narrow, [VMEM] * 2, VMEM, (vectors, other), 1)
     else:
         whole = lax.all_gather(vectors, "sub", axis=0, tiled=True)
     m0, m1, m2, before = call(
@@ -348,14 +348,15 @@
         [pltpu.VMEM((BW + 1, width, rows_dev), F32)],
     )
     if pair:
-        whole2, across, m1 = call(
+        whole2, across = call(
             join_below_kernel,
             "join_below",
-            [narrow] * 2 + [block],
-            [VMEM] * 4,
+            [narrow] * 2,
             [VMEM] * 3,
-            (below, swap_sub(below), whole, m1),
+            [VMEM] * 2,
+            (below, swap_sub(below), whole),
             1,
+            flops=20_000_000_000,
         )
     else:
         whole2 = shifted(whole, BW)

time: 41.8 us -> 41 us (0.981)
  starting transfers between devices: 21.6 us -> 18.7 us
  waiting for transfers between devices: 10.5 us -> 13.3 us
  other arithmetic: 0.69 us -> 0.03 us
    ppermute x4, waiting for transfers between devices: 0.01 us -> 2.66 us  [swap_sub(): return lax.ppermute(value, 'sub', [(0, 1), (1, 0)])]
    ppermute x2, starting transfers between devices: 6.13 us -> 4.68 us  [shifted(): lax.ppermute(value, 'blk', [(source, source + steps) for source in range(...]
    ppermute x5, waiting for transfers between devices: 7.71 us -> 8.77 us  [run_rounds(): total = total + lax.ppermute(value, axis, pairs)]
    add x1, other arithmetic: 0.66 us -> 0.01 us  [on_device(): tile_rows + LIVE_UNIT * tile_count]
    ppermute x2, waiting for transfers between devices: 1.4 us -> 0.79 us  [swap_core(): lax.ppermute(value, 'blk', [(i, i ^ 1) for i in range(lax.axis_size('blk'...]
    ppermute x5, starting transfers between devices: 9.68 us -> 9.17 us  [run_rounds(): total = total + lax.ppermute(value, axis, pairs)]
    ppermute x2, starting transfers between devices: 0.57 us -> 0.1 us  [swap_core(): lax.ppermute(value, 'blk', [(i, i ^ 1) for i in range(lax.axis_size('blk'...]
    ppermute x4, starting transfers between devices: 5.23 us -> 4.78 us  [swap_sub(): return lax.ppermute(value, 'sub', [(0, 1), (1, 0)])]
  transfers between devices with their start and end apart: 13 -> 13, of which waited for: 8 -> 9; matrix products, arithmetic and copies ran while one was open for 2% -> 0% of each run, Pallas kernels for 17% -> 18%
where the time goes in v1:
time: 41 us; the launch traced here: 40.8 us
  starting transfers between devices  18.7 us (46%)
  waiting for transfers between devices  13.3 us (32%)
  Pallas kernels  7.93 us (19%)
  between operations  0.83 us (2%)
    ppermute x5, starting transfers between devices, run_rounds(): total = total + lax.ppermute(value, axis, pairs)  9.17 us
    ppermute x5, waiting for transfers between devices, run_rounds(): total = total + lax.ppermute(value, axis, pairs)  8.77 us
    pallas_call x9, Pallas kernels, call(): pl.pallas_call(kernel, out_shape=out_shape, in_specs=in_specs, out_specs=...  7.93 us
    ppermute x4, starting transfers between devices, swap_sub(): return lax.ppermute(value, 'sub', [(0, 1), (1, 0)])  4.78 us
    ppermute x2, starting transfers between devices, shifted(): lax.ppermute(value, 'blk', [(source, source + steps) for source in range(...  4.68 us
    ppermute x4, waiting for transfers between devices, swap_sub(): return lax.ppermute(value, 'sub', [(0, 1), (1, 0)])  2.66 us
    ppermute x2, waiting for transfers between devices, shifted(): lax.ppermute(value, 'blk', [(source, source + steps) for source in range(...  1.08 us
  transfers between devices with their start and end apart: 13, of which 9 were waited for; matrix products, arithmetic and copies ran while one was open for 0% of the time, Pallas kernels for 18%

profile of v1, /device:TPU:0, one launch (start us, length us, event | category | flops | bytes accessed | tf_op | source)
XLA Modules:
  0.0 40.8 jit_solution(1569032681455616044)
XLA Ops:
  0.0 3.0 %collective-permute-start = (bf16[8,8192]{1,0:T(8,128)(2,1)}, bf16[8,8192]{1,0:T(8,128)(2,1)S(1)}, u32[]{:S(2)}, u32[]{:S(2)}) collective-permute-start(bf16[8,8192]{1,0:T(8,128)(2,1)} %mine.1), channel_id=1, source_target_pairs={{0,1},{1,0},{2,3},{3,2},{4,5},{5,4},{6,7},{7,6},{8,9},{9,8},{10,11... | collective-permute-start | bytes 393224 | tf_op jit(solution)/shard_map/ppermute | solution.py:30
  3.0 3.4 %collective-permute-start.1 = (bf16[8,8192]{1,0:T(8,128)(2,1)}, bf16[8,8192]{1,0:T(8,128)(2,1)S(1)}, u32[]{:S(2)}, u32[]{:S(2)}) collective-permute-start(bf16[8,8192]{1,0:T(8,128)(2,1)} %mine.1), channel_id=1, source_target_pairs={{0,4},{2,6},{4,8},{6,10},{8,12},{10,14},{12,16},{14,18},{16,20},{1... | collective-permute-start | bytes 393224 | tf_op jit(solution)/shard_map/ppermute | solution.py:26
  6.4 1.6 %load.1.tiles = bf16[64,128,128]{2,1,0:T(8,128)(2,1)S(1)} custom-call(bf16[64,128,128]{2,1,0:T(8,128)(2,1)} %bitcast.5), custom_call_target="tpu_custom_call" | custom-call | flops 20000000000 | bytes 3000000 | tf_op jit(solution)/shard_map/load/pallas_call | solution.py:292
  8.7 0.5 %collective-permute-done.1.own = bf16[8,8192]{1,0:T(8,128)(2,1)S(1)} collective-permute-done((bf16[8,8192]{1,0:T(8,128)(2,1)}, bf16[8,8192]{1,0:T(8,128)(2,1)S(1)}, u32[]{:S(2)}, u32[]{:S(2)}) %collective-permute-start.1) | collective-permute-done | bytes 131104 | tf_op jit(solution)/shard_map/ppermute | solution.py:26
  9.2 0.5 %collective-permute-start.2 = (bf16[8,8192]{1,0:T(8,128)(2,1)S(1)}, bf16[8,8192]{1,0:T(8,128)(2,1)S(1)}, u32[]{:S(2)}, u32[]{:S(2)}) collective-permute-start(bf16[8,8192]{1,0:T(8,128)(2,1)S(1)} %collective-permute-done.1.own), channel_id=1, source_target_pairs={{0,1},{1,0},{2,3},{3,2},{4,5},{5,4},{6,7},{7,6},{8,9},{9,8},{10,11... | collective-permute-start | bytes 393224 | tf_op jit(solution)/shard_map/ppermute | solution.py:30
  9.8 1.7 %mirror.1 = (f32[16,8192]{1,0:T(8,128)S(1)}, f32[16,8192]{1,0:T(8,128)S(1)}, f32[16,8192]{1,0:T(8,128)S(1)}, f32[32,128]{1,0:T(8,128)S(1)}) custom-call(s32[3,64]{1,0:T(4,128)S(1)} %pad_add_fusion.table, bf16[16,8192]{1,0:T(8,128)(2,1)S(1)} %join.1.whole.vec, f32[64,128]{1,0:T(8,128)S(1)} %bitcast.3, bf16[64,128,128]{2,1,0:T(8,128)(2,1)S(1)} %load.1.tiles), custom_call_target="tpu_custom_call" | custom-call | bytes 6000000 | tf_op jit(solution)/shard_map/mirror/pallas_call | solution.py:292
  11.5 2.7 %collective-permute-done.2.other = bf16[8,8192]{1,0:T(8,128)(2,1)S(1)} collective-permute-done((bf16[8,8192]{1,0:T(8,128)(2,1)S(1)}, bf16[8,8192]{1,0:T(8,128)(2,1)S(1)}, u32[]{:S(2)}, u32[]{:S(2)}) %collective-permute-start.2) | collective-permute-done | bytes 131104 | tf_op jit(solution)/shard_map/ppermute | solution.py:30
  14.4 0.7 %collective-permute-start.11 = (f32[8,8192]{1,0:T(8,128)S(1)}, f32[8,8192]{1,0:T(8,128)S(1)}, u32[]{:S(2)}, u32[]{:S(2)}) collective-permute-start(f32[8,8192]{1,0:T(8,128)S(1)} %get-tuple-element.26), channel_id=1, source_target_pairs={{0,1},{1,0},{2,3},{3,2},{4,5},{5,4},{6,7},{7,6},{8,9},{9,8},{10,11... | collective-permute-start | bytes 786440 | tf_op jit(solution)/shard_map/ppermute | solution.py:30
  15.0 0.8 %collective-permute-done.3.vec1 = bf16[16,8192]{1,0:T(8,128)(2,1)S(1)} collective-permute-done((bf16[16,8192]{1,0:T(8,128)(2,1)S(1)}, bf16[16,8192]{1,0:T(8,128)(2,1)S(1)}, u32[]{:S(2)}, u32[]{:S(2)}) %collective-permute-start.3) | collective-permute-done | bytes 262176 | tf_op jit(solution)/shard_map/ppermute | solution.py:34
  15.8 2.4 %direct.1 = (f32[8,8192]{1,0:T(8,128)S(1)}, f32[8,8192]{1,0:T(8,128)S(1)}, f32[32,128]{1,0:T(8,128)S(1)}) custom-call(s32[3,64]{1,0:T(4,128)S(1)} %pad_add_fusion.table, bf16[16,8192]{1,0:T(8,128)(2,1)S(1)} %join.1.whole.vec, bf16[16,8192]{1,0:T(8,128)(2,1)S(1)} %collective-permute-done.3.vec1, bf16[16,8192]{1,0:T(8,128)(2,1)S(1)} %get-tuple-element.17.vec2, ...), custom_call_target="tpu_custom_call" | custom-call | bytes 9000000 | tf_op jit(solution)/shard_map/direct/pallas_call | solution.py:292
  18.2 2.4 %collective-permute-start.5 = (f32[32,128]{1,0:T(8,128)S(1)}, f32[32,128]{1,0:T(8,128)S(1)}, u32[]{:S(2)}, u32[]{:S(2)}) collective-permute-start(f32[32,128]{1,0:T(8,128)S(1)} %get-tuple-element.21), channel_id=1, source_target_pairs={{0,4},{2,6},{4,0},{6,2},{8,12},{10,14},{12,8},{14,10},{16,20},{18,... | collective-permute-start | bytes 49160 | tf_op jit(solution)/shard_map/ppermute | solution.py:56
  20.6 1.7 %collective-permute-done.5 = f32[32,128]{1,0:T(8,128)S(1)} collective-permute-done((f32[32,128]{1,0:T(8,128)S(1)}, f32[32,128]{1,0:T(8,128)S(1)}, u32[]{:S(2)}, u32[]{:S(2)}) %collective-permute-start.5) | collective-permute-done | bytes 16416 | tf_op jit(solution)/shard_map/ppermute | solution.py:56
  22.3 3.0 %collective-permute-start.6 = (f32[32,128]{1,0:T(8,128)S(1)}, f32[32,128]{1,0:T(8,128)S(1)}, u32[]{:S(2)}, u32[]{:S(2)}) collective-permute-start(f32[32,128]{1,0:T(8,128)S(1)} %add.28), channel_id=1, source_target_pairs={{0,8},{2,10},{4,12},{6,14},{8,0},{10,2},{12,4},{14,6},{16,24},{18,... | collective-permute-start | bytes 49160 | tf_op jit(solution)/shard_map/ppermute | solution.py:56
  25.3 1.7 %collective-permute-done.6 = f32[32,128]{1,0:T(8,128)S(1)} collective-permute-done((f32[32,128]{1,0:T(8,128)S(1)}, f32[32,128]{1,0:T(8,128)S(1)}, u32[]{:S(2)}, u32[]{:S(2)}) %collective-permute-start.6) | collective-permute-done | bytes 16416 | tf_op jit(solution)/shard_map/ppermute | solution.py:56
  27.0 3.0 %collective-permute-start.7 = (f32[32,128]{1,0:T(8,128)S(1)}, f32[32,128]{1,0:T(8,128)S(1)}, u32[]{:S(2)}, u32[]{:S(2)}) collective-permute-start(f32[32,128]{1,0:T(8,128)S(1)} %add.29), channel_id=1, source_target_pairs={{0,16},{2,18},{4,20},{6,22},{8,24},{10,26},{12,28},{14,30},{16,0},... | collective-permute-start | bytes 49160 | tf_op jit(solution)/shard_map/ppermute | solution.py:56
  30.1 0.6 %collective-permute-start.10 = (f32[8,8192]{1,0:T(8,128)S(1)}, f32[8,8192]{1,0:T(8,128)S(1)}, u32[]{:S(2)}, u32[]{:S(2)}) collective-permute-start(f32[8,8192]{1,0:T(8,128)S(1)} %get-tuple-element.23), channel_id=1, source_target_pairs={{0,1},{1,0},{2,3},{3,2},{4,5},{5,4},{6,7},{7,6},{8,9},{9,8},{10,11... | collective-permute-start | bytes 786440 | tf_op jit(solution)/shard_map/ppermute | solution.py:30
  30.7 1.1 %collective-permute-done.7 = f32[32,128]{1,0:T(8,128)S(1)} collective-permute-done((f32[32,128]{1,0:T(8,128)S(1)}, f32[32,128]{1,0:T(8,128)S(1)}, u32[]{:S(2)}, u32[]{:S(2)}) %collective-permute-start.7) | collective-permute-done | bytes 16416 | tf_op jit(solution)/shard_map/ppermute | solution.py:56
  31.8 1.3 %collective-permute-start.12 = (f32[8,8192]{1,0:T(8,128)S(1)}, f32[8,8192]{1,0:T(8,128)S(1)}, u32[]{:S(2)}, u32[]{:S(2)}) collective-permute-start(f32[8,8192]{1,0:T(8,128)S(1)} %sum.1), channel_id=1, source_target_pairs={{4,0},{6,2},{8,4},{10,6},{12,8},{14,10},{16,12},{18,14},{20,16},{2... | collective-permute-start | bytes 786440 | tf_op jit(solution)/shard_map/ppermute | solution.py:26
  33.2 1.2 %collective-permute-done.8 = f32[32,128]{1,0:T(8,128)S(1)} collective-permute-done((f32[32,128]{1,0:T(8,128)S(1)}, f32[32,128]{1,0:T(8,128)S(1)}, u32[]{:S(2)}, u32[]{:S(2)}) %collective-permute-start.8) | collective-permute-done | bytes 16416 | tf_op jit(solution)/shard_map/ppermute | solution.py:56
  34.4 0.6 %collective-permute-start.9 = (f32[32,128]{1,0:T(8,128)S(1)}, f32[32,128]{1,0:T(8,128)S(1)}, u32[]{:S(2)}, u32[]{:S(2)}) collective-permute-start(f32[32,128]{1,0:T(8,128)S(1)} %add.31), channel_id=1, source_target_pairs={{0,1},{1,0},{2,3},{3,2},{4,5},{5,4},{6,7},{7,6},{8,9},{9,8},{10,11... | collective-permute-start | bytes 49160 | tf_op jit(solution)/shard_map/ppermute | solution.py:56
  35.0 3.1 %collective-permute-done.9 = f32[32,128]{1,0:T(8,128)S(1)} collective-permute-done((f32[32,128]{1,0:T(8,128)S(1)}, f32[32,128]{1,0:T(8,128)S(1)}, u32[]{:S(2)}, u32[]{:S(2)}) %collective-permute-start.9) | collective-permute-done | bytes 16416 | tf_op jit(solution)/shard_map/ppermute | solution.py:56
  38.1 1.3 %model.1.first = f32[8,8192]{1,0:T(8,128)S(1)} custom-call(f32[32,128]{1,0:T(8,128)S(1)} %add.32.small, bf16[16,8192]{1,0:T(8,128)(2,1)S(1)} %join.1.whole.vec, bf16[8,8192]{1,0:T(8,128)(2,1)S(1)} %copy-done, f32[64,128]{1,0:T(8,128)S(1)} %bitcast.4, f32[8,8192]{1,0:T(8,128)S(1)} %get-tuple-element.22.rest_0_, f32[8,8192]{1,0:T(8,128)S(1)} %collective-permute-done.10.rest_1_), custom_call_target="tpu_custom_call" | custom-call | bytes 6000000 | tf_op jit(solution)/shard_map/model/pallas_call | solution.py:292
  39.5 0.6 %collective-permute-done.12.second = f32[8,8192]{1,0:T(8,128)S(1)} collective-permute-done((f32[8,8192]{1,0:T(8,128)S(1)}, f32[8,8192]{1,0:T(8,128)S(1)}, u32[]{:S(2)}, u32[]{:S(2)}) %collective-permute-start.12) | collective-permute-done | bytes 262176 | tf_op jit(solution)/shard_map/ppermute | solution.py:26
  40.1 0.7 %last.1 = f32[8,8192]{1,0:T(8,128)} custom-call(f32[8,8192]{1,0:T(8,128)S(1)} %model.1.first, f32[8,8192]{1,0:T(8,128)S(1)} %collective-permute-done.12.second), custom_call_target="tpu_custom_call" | custom-call | bytes 3000000 | tf_op jit(solution)/shard_map/last/pallas_call | solution.py:292
  (28 shorter events, 0.4 us)
Async XLA Ops:
  0.0 9.7 %collective-permute-start = (bf16[8,8192]{1,0:T(8,128)(2,1)}, bf16[8,8192]{1,0:T(8,128)(2,1)S(1)}, u32[]{:S(2)}, u32[]{:S(2)}) collective-permute-start(bf16[8,8192]{1,0:T(8,128)(2,1)} %mine.1), channel_id=1, source_target_pairs={{0,1},{1,0},{2,3},{3,2},{4,5},{5,4},{6,7},{7,6},{8,9},{9,8},{10,11... | collective-permute-start | bytes 393224 | tf_op jit(solution)/shard_map/ppermute | solution.py:30
  3.0 6.2 %collective-permute-start.1 = (bf16[8,8192]{1,0:T(8,128)(2,1)}, bf16[8,8192]{1,0:T(8,128)(2,1)S(1)}, u32[]{:S(2)}, u32[]{:S(2)}) collective-permute-start(bf16[8,8192]{1,0:T(8,128)(2,1)} %mine.1), channel_id=1, source_target_pairs={{0,4},{2,6},{4,8},{6,10},{8,12},{10,14},{12,16},{14,18},{16,20},{1... | collective-permute-start | bytes 393224 | tf_op jit(solution)/shard_map/ppermute | solution.py:26
  6.4 3.3 %copy-start.4 = (s32[1,64]{1,0:T(1,128)S(1)}, s32[1,64]{1,0:T(1,128)}, u32[]{:S(2)}) copy-start(s32[1,64]{1,0:T(1,128)} %param.10) | copy-start | bytes 772
  6.4 3.3 %copy-start.2 = (s32[1,64]{1,0:T(1,128)S(1)}, s32[1,64]{1,0:T(1,128)}, u32[]{:S(2)}) copy-start(s32[1,64]{1,0:T(1,128)} %param.12) | copy-start | bytes 772
  6.4 3.3 %copy-start.3 = (s32[1,64]{1,0:T(1,128)S(1)}, s32[1,64]{1,0:T(1,128)}, u32[]{:S(2)}) copy-start(s32[1,64]{1,0:T(1,128)} %param.11) | copy-start | bytes 772
  6.4 3.3 %copy-start = (bf16[8,8192]{1,0:T(8,128)(2,1)S(1)}, bf16[8,8192]{1,0:T(8,128)(2,1)}, u32[]{:S(2)}) copy-start(bf16[8,8192]{1,0:T(8,128)(2,1)} %mine.1) | copy-start | bytes 393220
  6.4 3.4 %copy-start.1 = (f32[8192]{0:T(1024)S(1)}, f32[8192]{0:T(1024)}, u32[]{:S(2)}) copy-start(f32[8192]{0:T(1024)} %param.8) | copy-start | bytes 98308
  9.2 5.0 %collective-permute-start.2 = (bf16[8,8192]{1,0:T(8,128)(2,1)S(1)}, bf16[8,8192]{1,0:T(8,128)(2,1)S(1)}, u32[]{:S(2)}, u32[]{:S(2)}) collective-permute-start(bf16[8,8192]{1,0:T(8,128)(2,1)S(1)} %collective-permute-done.1.own), channel_id=1, source_target_pairs={{0,1},{1,0},{2,3},{3,2},{4,5},{5,4},{6,7},{7,6},{8,9},{9,8},{10,11... | collective-permute-start | bytes 393224 | tf_op jit(solution)/shard_map/ppermute | solution.py:30
  11.5 2.8 %collective-permute-start.4 = (f32[16,8192]{1,0:T(8,128)S(1)}, f32[16,8192]{1,0:T(8,128)S(1)}, u32[]{:S(2)}, u32[]{:S(2)}) collective-permute-start(f32[16,8192]{1,0:T(8,128)S(1)} %get-tuple-element.19), channel_id=1, source_target_pairs={{0,2},{2,0},{4,6},{6,4},{8,10},{10,8},{12,14},{14,12},{16,18},{18,... | collective-permute-start | bytes 1572872 | tf_op jit(solution)/shard_map/ppermute | solution.py:34
  14.2 1.6 %collective-permute-start.3 = (bf16[16,8192]{1,0:T(8,128)(2,1)S(1)}, bf16[16,8192]{1,0:T(8,128)(2,1)S(1)}, u32[]{:S(2)}, u32[]{:S(2)}) collective-permute-start(bf16[16,8192]{1,0:T(8,128)(2,1)S(1)} %get-tuple-element.16), channel_id=1, source_target_pairs={{0,2},{2,0},{4,6},{6,4},{8,10},{10,8},{12,14},{14,12},{16,18},{18,... | collective-permute-start | bytes 786440 | tf_op jit(solution)/shard_map/ppermute | solution.py:34
  14.4 17.4 %collective-permute-start.11 = (f32[8,8192]{1,0:T(8,128)S(1)}, f32[8,8192]{1,0:T(8,128)S(1)}, u32[]{:S(2)}, u32[]{:S(2)}) collective-permute-start(f32[8,8192]{1,0:T(8,128)S(1)} %get-tuple-element.26), channel_id=1, source_target_pairs={{0,1},{1,0},{2,3},{3,2},{4,5},{5,4},{6,7},{7,6},{8,9},{9,8},{10,11... | collective-permute-start | bytes 786440 | tf_op jit(solution)/shard_map/ppermute | solution.py:30
  18.2 4.1 %collective-permute-start.5 = (f32[32,128]{1,0:T(8,128)S(1)}, f32[32,128]{1,0:T(8,128)S(1)}, u32[]{:S(2)}, u32[]{:S(2)}) collective-permute-start(f32[32,128]{1,0:T(8,128)S(1)} %get-tuple-element.21), channel_id=1, source_target_pairs={{0,4},{2,6},{4,0},{6,2},{8,12},{10,14},{12,8},{14,10},{16,20},{18,... | collective-permute-start | bytes 49160 | tf_op jit(solution)/shard_map/ppermute | solution.py:56
  22.3 4.7 %collective-permute-start.6 = (f32[32,128]{1,0:T(8,128)S(1)}, f32[32,128]{1,0:T(8,128)S(1)}, u32[]{:S(2)}, u32[]{:S(2)}) collective-permute-start(f32[32,128]{1,0:T(8,128)S(1)} %add.28), channel_id=1, source_target_pairs={{0,8},{2,10},{4,12},{6,14},{8,0},{10,2},{12,4},{14,6},{16,24},{18,... | collective-permute-start | bytes 49160 | tf_op jit(solution)/shard_map/ppermute | solution.py:56
  27.0 4.8 %collective-permute-start.7 = (f32[32,128]{1,0:T(8,128)S(1)}, f32[32,128]{1,0:T(8,128)S(1)}, u32[]{:S(2)}, u32[]{:S(2)}) collective-permute-start(f32[32,128]{1,0:T(8,128)S(1)} %add.29), channel_id=1, source_target_pairs={{0,16},{2,18},{4,20},{6,22},{8,24},{10,26},{12,28},{14,30},{16,0},... | collective-permute-start | bytes 49160 | tf_op jit(solution)/shard_map/ppermute | solution.py:56
  30.1 8.1 %collective-permute-start.10 = (f32[8,8192]{1,0:T(8,128)S(1)}, f32[8,8192]{1,0:T(8,128)S(1)}, u32[]{:S(2)}, u32[]{:S(2)}) collective-permute-start(f32[8,8192]{1,0:T(8,128)S(1)} %get-tuple-element.23), channel_id=1, source_target_pairs={{0,1},{1,0},{2,3},{3,2},{4,5},{5,4},{6,7},{7,6},{8,9},{9,8},{10,11... | collective-permute-start | bytes 786440 | tf_op jit(solution)/shard_map/ppermute | solution.py:30
  31.8 8.3 %collective-permute-start.12 = (f32[8,8192]{1,0:T(8,128)S(1)}, f32[8,8192]{1,0:T(8,128)S(1)}, u32[]{:S(2)}, u32[]{:S(2)}) collective-permute-start(f32[8,8192]{1,0:T(8,128)S(1)} %sum.1), channel_id=1, source_target_pairs={{4,0},{6,2},{8,4},{10,6},{12,8},{14,10},{16,12},{18,14},{20,16},{2... | collective-permute-start | bytes 786440 | tf_op jit(solution)/shard_map/ppermute | solution.py:26
  33.1 1.2 %collective-permute-start.8 = (f32[32,128]{1,0:T(8,128)S(1)}, f32[32,128]{1,0:T(8,128)S(1)}, u32[]{:S(2)}, u32[]{:S(2)}) collective-permute-start(f32[32,128]{1,0:T(8,128)S(1)} %add.30.ready), channel_id=1, source_target_pairs={{0,2},{2,0},{4,6},{6,4},{8,10},{10,8},{12,14},{14,12},{16,18},{18,... | collective-permute-start | bytes 49160 | tf_op jit(solution)/shard_map/ppermute | solution.py:56
  34.4 3.7 %collective-permute-start.9 = (f32[32,128]{1,0:T(8,128)S(1)}, f32[32,128]{1,0:T(8,128)S(1)}, u32[]{:S(2)}, u32[]{:S(2)}) collective-permute-start(f32[32,128]{1,0:T(8,128)S(1)} %add.31), channel_id=1, source_target_pairs={{0,1},{1,0},{2,3},{3,2},{4,5},{5,4},{6,7},{7,6},{8,9},{9,8},{10,11... | collective-permute-start | bytes 49160 | tf_op jit(solution)/shard_map/ppermute | solution.py:56

commit v2 on v1

--- a/solution.py
+++ b/solution.py
@@ -264,12 +264,12 @@
 
 
 def model_kernel(small, vec, mine, energies, *rest):
-    terms, (out, coeffs) = rest[:-2], rest[-2:]
+    terms, out = rest[:-1], rest[-1]
     width, rows_dev = vec.shape
     columns = mine.shape[0]
     side = energies.shape[1]
-    coeffs[...] = eliminate(small[:, :width])
-    wanted = coeffs[pl.ds(lax.axis_index("sub") * columns, columns), :]
+    own = pl.ds(width + lax.axis_index("sub") * columns, columns)
+    wanted = eliminate(jnp.concatenate([small[0:width, :], small[own, :]], 0)[:, :width])
     high, rest_of = split2(wanted)
     mid, low = split2(rest_of)
     factors = jnp.concatenate([high, mid, low], 0).astype(BF16)
@@ -282,10 +282,6 @@
         for term in terms:
             applied = applied + term[:, here]
         out[:, here] = applied - model
-
-
-def last_kernel(first, second, out):
-    out[...] = first[...] + second[...]
 
 
 def call(kernel, name, out_shape, in_specs, out_specs, args, cycles, scratch=(), room=24, flops=0):
@@ -410,9 +406,8 @@
         VMEM,
         (small, whole, vectors, levels, *terms),
         2,
-        [pltpu.VMEM((width, width), F32)],
-    )
-    return call(last_kernel, "last", half, [VMEM] * 2, VMEM, (nearly, shifted(up, -BW)), 1)
+    )
+    return nearly + shifted(up, -BW)
 
 
 def solution(mesh):

time: 41 us -> 41 us (level)
  Pallas kernels: 7.93 us -> 7.19 us
  other arithmetic: 0.03 us -> 0.76 us
    pallas_call x9 -> x8, Pallas kernels: 7.93 us -> 7.19 us  [call(): pl.pallas_call(kernel, out_shape=out_shape, in_specs=in_specs, out_specs=...]
    add x0 -> x1, other arithmetic: none -> 0.73 us  [on_device(): return nearly + shifted(up, -BW)]
where the time goes in v2:
time: 41 us; the launch traced here: 40.8 us
  starting transfers between devices  18.8 us (46%)
  waiting for transfers between devices  13.3 us (32%)
  Pallas kernels  7.19 us (18%)
  between operations  0.83 us (2%)
  other arithmetic  0.76 us (2%)
    ppermute x5, starting transfers between devices, run_rounds(): total = total + lax.ppermute(value, axis, pairs)  9.16 us
    ppermute x5, waiting for transfers between devices, run_rounds(): total = total + lax.ppermute(value, axis, pairs)  8.76 us
    pallas_call x8, Pallas kernels, call(): pl.pallas_call(kernel, out_shape=out_shape, in_specs=in_specs, out_specs=...  7.19 us
    ppermute x4, starting transfers between devices, swap_sub(): return lax.ppermute(value, 'sub', [(0, 1), (1, 0)])  4.81 us
    ppermute x2, starting transfers between devices, shifted(): lax.ppermute(value, 'blk', [(source, source + steps) for source in range(...  4.68 us
    ppermute x4, waiting for transfers between devices, swap_sub(): return lax.ppermute(value, 'sub', [(0, 1), (1, 0)])  2.66 us
    ppermute x2, waiting for transfers between devices, shifted(): lax.ppermute(value, 'blk', [(source, source + steps) for source in range(...  1.09 us
  transfers between devices with their start and end apart: 13, of which 9 were waited for; matrix products, arithmetic and copies ran while one was open for 0% of the time, Pallas kernels for 18%

profile of v2, /device:TPU:0, one launch (start us, length us, event | category | flops | bytes accessed | tf_op | source)
XLA Modules:
  0.0 40.8 jit_solution(6575156496940122881)
XLA Ops:
  0.0 3.0 %collective-permute-start = (bf16[8,8192]{1,0:T(8,128)(2,1)}, bf16[8,8192]{1,0:T(8,128)(2,1)S(1)}, u32[]{:S(2)}, u32[]{:S(2)}) collective-permute-start(bf16[8,8192]{1,0:T(8,128)(2,1)} %mine.1), channel_id=1, source_target_pairs={{0,1},{1,0},{2,3},{3,2},{4,5},{5,4},{6,7},{7,6},{8,9},{9,8},{10,11... | collective-permute-start | bytes 393224 | tf_op jit(solution)/shard_map/ppermute | solution.py:30
  3.0 3.4 %collective-permute-start.1 = (bf16[8,8192]{1,0:T(8,128)(2,1)}, bf16[8,8192]{1,0:T(8,128)(2,1)S(1)}, u32[]{:S(2)}, u32[]{:S(2)}) collective-permute-start(bf16[8,8192]{1,0:T(8,128)(2,1)} %mine.1), channel_id=1, source_target_pairs={{0,4},{2,6},{4,8},{6,10},{8,12},{10,14},{12,16},{14,18},{16,20},{1... | collective-permute-start | bytes 393224 | tf_op jit(solution)/shard_map/ppermute | solution.py:26
  6.4 1.6 %load.1.tiles = bf16[64,128,128]{2,1,0:T(8,128)(2,1)S(1)} custom-call(bf16[64,128,128]{2,1,0:T(8,128)(2,1)} %bitcast.5), custom_call_target="tpu_custom_call" | custom-call | flops 20000000000 | bytes 3000000 | tf_op jit(solution)/shard_map/load/pallas_call | solution.py:288
  8.7 0.5 %collective-permute-done.1.own = bf16[8,8192]{1,0:T(8,128)(2,1)S(1)} collective-permute-done((bf16[8,8192]{1,0:T(8,128)(2,1)}, bf16[8,8192]{1,0:T(8,128)(2,1)S(1)}, u32[]{:S(2)}, u32[]{:S(2)}) %collective-permute-start.1) | collective-permute-done | bytes 131104 | tf_op jit(solution)/shard_map/ppermute | solution.py:26
  9.2 0.5 %collective-permute-start.2 = (bf16[8,8192]{1,0:T(8,128)(2,1)S(1)}, bf16[8,8192]{1,0:T(8,128)(2,1)S(1)}, u32[]{:S(2)}, u32[]{:S(2)}) collective-permute-start(bf16[8,8192]{1,0:T(8,128)(2,1)S(1)} %collective-permute-done.1.own), channel_id=1, source_target_pairs={{0,1},{1,0},{2,3},{3,2},{4,5},{5,4},{6,7},{7,6},{8,9},{9,8},{10,11... | collective-permute-start | bytes 393224 | tf_op jit(solution)/shard_map/ppermute | solution.py:30
  9.8 1.7 %mirror.1 = (f32[16,8192]{1,0:T(8,128)S(1)}, f32[16,8192]{1,0:T(8,128)S(1)}, f32[16,8192]{1,0:T(8,128)S(1)}, f32[32,128]{1,0:T(8,128)S(1)}) custom-call(s32[3,64]{1,0:T(4,128)S(1)} %pad_add_fusion.table, bf16[16,8192]{1,0:T(8,128)(2,1)S(1)} %join.1.whole.vec, f32[64,128]{1,0:T(8,128)S(1)} %bitcast.3, bf16[64,128,128]{2,1,0:T(8,128)(2,1)S(1)} %load.1.tiles), custom_call_target="tpu_custom_call" | custom-call | bytes 6000000 | tf_op jit(solution)/shard_map/mirror/pallas_call | solution.py:288
  11.5 2.6 %collective-permute-done.2.other = bf16[8,8192]{1,0:T(8,128)(2,1)S(1)} collective-permute-done((bf16[8,8192]{1,0:T(8,128)(2,1)S(1)}, bf16[8,8192]{1,0:T(8,128)(2,1)S(1)}, u32[]{:S(2)}, u32[]{:S(2)}) %collective-permute-start.2) | collective-permute-done | bytes 131104 | tf_op jit(solution)/shard_map/ppermute | solution.py:30
  14.4 0.7 %collective-permute-start.11 = (f32[8,8192]{1,0:T(8,128)S(1)}, f32[8,8192]{1,0:T(8,128)S(1)}, u32[]{:S(2)}, u32[]{:S(2)}) collective-permute-start(f32[8,8192]{1,0:T(8,128)S(1)} %get-tuple-element.26), channel_id=1, source_target_pairs={{0,1},{1,0},{2,3},{3,2},{4,5},{5,4},{6,7},{7,6},{8,9},{9,8},{10,11... | collective-permute-start | bytes 786440 | tf_op jit(solution)/shard_map/ppermute | solution.py:30
  15.1 0.8 %collective-permute-done.3.vec1 = bf16[16,8192]{1,0:T(8,128)(2,1)S(1)} collective-permute-done((bf16[16,8192]{1,0:T(8,128)(2,1)S(1)}, bf16[16,8192]{1,0:T(8,128)(2,1)S(1)}, u32[]{:S(2)}, u32[]{:S(2)}) %collective-permute-start.3) | collective-permute-done | bytes 262176 | tf_op jit(solution)/shard_map/ppermute | solution.py:34
  15.8 2.4 %direct.1 = (f32[8,8192]{1,0:T(8,128)S(1)}, f32[8,8192]{1,0:T(8,128)S(1)}, f32[32,128]{1,0:T(8,128)S(1)}) custom-call(s32[3,64]{1,0:T(4,128)S(1)} %pad_add_fusion.table, bf16[16,8192]{1,0:T(8,128)(2,1)S(1)} %join.1.whole.vec, bf16[16,8192]{1,0:T(8,128)(2,1)S(1)} %collective-permute-done.3.vec1, bf16[16,8192]{1,0:T(8,128)(2,1)S(1)} %get-tuple-element.17.vec2, ...), custom_call_target="tpu_custom_call" | custom-call | bytes 9000000 | tf_op jit(solution)/shard_map/direct/pallas_call | solution.py:288
  18.2 2.4 %collective-permute-start.5 = (f32[32,128]{1,0:T(8,128)S(1)}, f32[32,128]{1,0:T(8,128)S(1)}, u32[]{:S(2)}, u32[]{:S(2)}) collective-permute-start(f32[32,128]{1,0:T(8,128)S(1)} %get-tuple-element.21), channel_id=1, source_target_pairs={{0,4},{2,6},{4,0},{6,2},{8,12},{10,14},{12,8},{14,10},{16,20},{18,... | collective-permute-start | bytes 49160 | tf_op jit(solution)/shard_map/ppermute | solution.py:56
  20.6 1.7 %collective-permute-done.5 = f32[32,128]{1,0:T(8,128)S(1)} collective-permute-done((f32[32,128]{1,0:T(8,128)S(1)}, f32[32,128]{1,0:T(8,128)S(1)}, u32[]{:S(2)}, u32[]{:S(2)}) %collective-permute-start.5) | collective-permute-done | bytes 16416 | tf_op jit(solution)/shard_map/ppermute | solution.py:56
  22.3 3.0 %collective-permute-start.6 = (f32[32,128]{1,0:T(8,128)S(1)}, f32[32,128]{1,0:T(8,128)S(1)}, u32[]{:S(2)}, u32[]{:S(2)}) collective-permute-start(f32[32,128]{1,0:T(8,128)S(1)} %add.31), channel_id=1, source_target_pairs={{0,8},{2,10},{4,12},{6,14},{8,0},{10,2},{12,4},{14,6},{16,24},{18,... | collective-permute-start | bytes 49160 | tf_op jit(solution)/shard_map/ppermute | solution.py:56
  25.3 1.7 %collective-permute-done.6 = f32[32,128]{1,0:T(8,128)S(1)} collective-permute-done((f32[32,128]{1,0:T(8,128)S(1)}, f32[32,128]{1,0:T(8,128)S(1)}, u32[]{:S(2)}, u32[]{:S(2)}) %collective-permute-start.6) | collective-permute-done | bytes 16416 | tf_op jit(solution)/shard_map/ppermute | solution.py:56
  27.0 3.0 %collective-permute-start.7 = (f32[32,128]{1,0:T(8,128)S(1)}, f32[32,128]{1,0:T(8,128)S(1)}, u32[]{:S(2)}, u32[]{:S(2)}) collective-permute-start(f32[32,128]{1,0:T(8,128)S(1)} %add.32), channel_id=1, source_target_pairs={{0,16},{2,18},{4,20},{6,22},{8,24},{10,26},{12,28},{14,30},{16,0},... | collective-permute-start | bytes 49160 | tf_op jit(solution)/shard_map/ppermute | solution.py:56
  30.1 0.6 %collective-permute-start.10 = (f32[8,8192]{1,0:T(8,128)S(1)}, f32[8,8192]{1,0:T(8,128)S(1)}, u32[]{:S(2)}, u32[]{:S(2)}) collective-permute-start(f32[8,8192]{1,0:T(8,128)S(1)} %get-tuple-element.23), channel_id=1, source_target_pairs={{0,1},{1,0},{2,3},{3,2},{4,5},{5,4},{6,7},{7,6},{8,9},{9,8},{10,11... | collective-permute-start | bytes 786440 | tf_op jit(solution)/shard_map/ppermute | solution.py:30
  30.7 1.1 %collective-permute-done.7 = f32[32,128]{1,0:T(8,128)S(1)} collective-permute-done((f32[32,128]{1,0:T(8,128)S(1)}, f32[32,128]{1,0:T(8,128)S(1)}, u32[]{:S(2)}, u32[]{:S(2)}) %collective-permute-start.7) | collective-permute-done | bytes 16416 | tf_op jit(solution)/shard_map/ppermute | solution.py:56
  31.8 1.3 %collective-permute-start.12 = (f32[8,8192]{1,0:T(8,128)S(1)}, f32[8,8192]{1,0:T(8,128)S(1)}, u32[]{:S(2)}, u32[]{:S(2)}) collective-permute-start(f32[8,8192]{1,0:T(8,128)S(1)} %sum.1), channel_id=1, source_target_pairs={{4,0},{6,2},{8,4},{10,6},{12,8},{14,10},{16,12},{18,14},{20,16},{2... | collective-permute-start | bytes 786440 | tf_op jit(solution)/shard_map/ppermute | solution.py:26
  33.2 1.2 %collective-permute-done.8 = f32[32,128]{1,0:T(8,128)S(1)} collective-permute-done((f32[32,128]{1,0:T(8,128)S(1)}, f32[32,128]{1,0:T(8,128)S(1)}, u32[]{:S(2)}, u32[]{:S(2)}) %collective-permute-start.8) | collective-permute-done | bytes 16416 | tf_op jit(solution)/shard_map/ppermute | solution.py:56
  34.4 0.6 %collective-permute-start.9 = (f32[32,128]{1,0:T(8,128)S(1)}, f32[32,128]{1,0:T(8,128)S(1)}, u32[]{:S(2)}, u32[]{:S(2)}) collective-permute-start(f32[32,128]{1,0:T(8,128)S(1)} %add.34), channel_id=1, source_target_pairs={{0,1},{1,0},{2,3},{3,2},{4,5},{5,4},{6,7},{7,6},{8,9},{9,8},{10,11... | collective-permute-start | bytes 49160 | tf_op jit(solution)/shard_map/ppermute | solution.py:56
  35.0 3.1 %collective-permute-done.9 = f32[32,128]{1,0:T(8,128)S(1)} collective-permute-done((f32[32,128]{1,0:T(8,128)S(1)}, f32[32,128]{1,0:T(8,128)S(1)}, u32[]{:S(2)}, u32[]{:S(2)}) %collective-permute-start.9) | collective-permute-done | bytes 16416 | tf_op jit(solution)/shard_map/ppermute | solution.py:56
  38.1 1.3 %model.1 = f32[8,8192]{1,0:T(8,128)S(1)} custom-call(f32[32,128]{1,0:T(8,128)S(1)} %add.35.small, bf16[16,8192]{1,0:T(8,128)(2,1)S(1)} %join.1.whole.vec, bf16[8,8192]{1,0:T(8,128)(2,1)S(1)} %copy-done, f32[64,128]{1,0:T(8,128)S(1)} %bitcast.4, f32[8,8192]{1,0:T(8,128)S(1)} %get-tuple-element.22.rest_0_, f32[8,8192]{1,0:T(8,128)S(1)} %collective-permute-done.10.rest_1_), custom_call_target="tpu_custom_call" | custom-call | bytes 6000000 | tf_op jit(solution)/shard_map/model/pallas_call | solution.py:288
  39.5 0.6 %collective-permute-done.12 = f32[8,8192]{1,0:T(8,128)S(1)} collective-permute-done((f32[8,8192]{1,0:T(8,128)S(1)}, f32[8,8192]{1,0:T(8,128)S(1)}, u32[]{:S(2)}, u32[]{:S(2)}) %collective-permute-start.12) | collective-permute-done | bytes 262176 | tf_op jit(solution)/shard_map/ppermute | solution.py:26
  40.1 0.7 %add.36 = f32[8,8192]{1,0:T(8,128)} add(f32[8,8192]{1,0:T(8,128)S(1)} %model.1, f32[8,8192]{1,0:T(8,128)S(1)} %collective-permute-done.12) | non-fusion elementwise | flops 65536 | bytes 786432 | tf_op jit(solution)/shard_map/add | solution.py:410
  (28 shorter events, 0.4 us)
Async XLA Ops:
  0.0 9.7 %collective-permute-start = (bf16[8,8192]{1,0:T(8,128)(2,1)}, bf16[8,8192]{1,0:T(8,128)(2,1)S(1)}, u32[]{:S(2)}, u32[]{:S(2)}) collective-permute-start(bf16[8,8192]{1,0:T(8,128)(2,1)} %mine.1), channel_id=1, source_target_pairs={{0,1},{1,0},{2,3},{3,2},{4,5},{5,4},{6,7},{7,6},{8,9},{9,8},{10,11... | collective-permute-start | bytes 393224 | tf_op jit(solution)/shard_map/ppermute | solution.py:30
  3.0 6.2 %collective-permute-start.1 = (bf16[8,8192]{1,0:T(8,128)(2,1)}, bf16[8,8192]{1,0:T(8,128)(2,1)S(1)}, u32[]{:S(2)}, u32[]{:S(2)}) collective-permute-start(bf16[8,8192]{1,0:T(8,128)(2,1)} %mine.1), channel_id=1, source_target_pairs={{0,4},{2,6},{4,8},{6,10},{8,12},{10,14},{12,16},{14,18},{16,20},{1... | collective-permute-start | bytes 393224 | tf_op jit(solution)/shard_map/ppermute | solution.py:26
  6.4 3.3 %copy-start.4 = (s32[1,64]{1,0:T(1,128)S(1)}, s32[1,64]{1,0:T(1,128)}, u32[]{:S(2)}) copy-start(s32[1,64]{1,0:T(1,128)} %param.10) | copy-start | bytes 772
  6.4 3.3 %copy-start.2 = (s32[1,64]{1,0:T(1,128)S(1)}, s32[1,64]{1,0:T(1,128)}, u32[]{:S(2)}) copy-start(s32[1,64]{1,0:T(1,128)} %param.12) | copy-start | bytes 772
  6.4 3.3 %copy-start.3 = (s32[1,64]{1,0:T(1,128)S(1)}, s32[1,64]{1,0:T(1,128)}, u32[]{:S(2)}) copy-start(s32[1,64]{1,0:T(1,128)} %param.11) | copy-start | bytes 772
  6.4 3.3 %copy-start = (bf16[8,8192]{1,0:T(8,128)(2,1)S(1)}, bf16[8,8192]{1,0:T(8,128)(2,1)}, u32[]{:S(2)}) copy-start(bf16[8,8192]{1,0:T(8,128)(2,1)} %mine.1) | copy-start | bytes 393220
  6.4 3.4 %copy-start.1 = (f32[8192]{0:T(1024)S(1)}, f32[8192]{0:T(1024)}, u32[]{:S(2)}) copy-start(f32[8192]{0:T(1024)} %param.8) | copy-start | bytes 98308
  9.2 5.0 %collective-permute-start.2 = (bf16[8,8192]{1,0:T(8,128)(2,1)S(1)}, bf16[8,8192]{1,0:T(8,128)(2,1)S(1)}, u32[]{:S(2)}, u32[]{:S(2)}) collective-permute-start(bf16[8,8192]{1,0:T(8,128)(2,1)S(1)} %collective-permute-done.1.own), channel_id=1, source_target_pairs={{0,1},{1,0},{2,3},{3,2},{4,5},{5,4},{6,7},{7,6},{8,9},{9,8},{10,11... | collective-permute-start | bytes 393224 | tf_op jit(solution)/shard_map/ppermute | solution.py:30
  11.5 2.8 %collective-permute-start.4 = (f32[16,8192]{1,0:T(8,128)S(1)}, f32[16,8192]{1,0:T(8,128)S(1)}, u32[]{:S(2)}, u32[]{:S(2)}) collective-permute-start(f32[16,8192]{1,0:T(8,128)S(1)} %get-tuple-element.19), channel_id=1, source_target_pairs={{0,2},{2,0},{4,6},{6,4},{8,10},{10,8},{12,14},{14,12},{16,18},{18,... | collective-permute-start | bytes 1572872 | tf_op jit(solution)/shard_map/ppermute | solution.py:34
  14.2 1.6 %collective-permute-start.3 = (bf16[16,8192]{1,0:T(8,128)(2,1)S(1)}, bf16[16,8192]{1,0:T(8,128)(2,1)S(1)}, u32[]{:S(2)}, u32[]{:S(2)}) collective-permute-start(bf16[16,8192]{1,0:T(8,128)(2,1)S(1)} %get-tuple-element.16), channel_id=1, source_target_pairs={{0,2},{2,0},{4,6},{6,4},{8,10},{10,8},{12,14},{14,12},{16,18},{18,... | collective-permute-start | bytes 786440 | tf_op jit(solution)/shard_map/ppermute | solution.py:34
  14.4 17.4 %collective-permute-start.11 = (f32[8,8192]{1,0:T(8,128)S(1)}, f32[8,8192]{1,0:T(8,128)S(1)}, u32[]{:S(2)}, u32[]{:S(2)}) collective-permute-start(f32[8,8192]{1,0:T(8,128)S(1)} %get-tuple-element.26), channel_id=1, source_target_pairs={{0,1},{1,0},{2,3},{3,2},{4,5},{5,4},{6,7},{7,6},{8,9},{9,8},{10,11... | collective-permute-start | bytes 786440 | tf_op jit(solution)/shard_map/ppermute | solution.py:30
  18.2 4.1 %collective-permute-start.5 = (f32[32,128]{1,0:T(8,128)S(1)}, f32[32,128]{1,0:T(8,128)S(1)}, u32[]{:S(2)}, u32[]{:S(2)}) collective-permute-start(f32[32,128]{1,0:T(8,128)S(1)} %get-tuple-element.21), channel_id=1, source_target_pairs={{0,4},{2,6},{4,0},{6,2},{8,12},{10,14},{12,8},{14,10},{16,20},{18,... | collective-permute-start | bytes 49160 | tf_op jit(solution)/shard_map/ppermute | solution.py:56
  22.3 4.7 %collective-permute-start.6 = (f32[32,128]{1,0:T(8,128)S(1)}, f32[32,128]{1,0:T(8,128)S(1)}, u32[]{:S(2)}, u32[]{:S(2)}) collective-permute-start(f32[32,128]{1,0:T(8,128)S(1)} %add.31), channel_id=1, source_target_pairs={{0,8},{2,10},{4,12},{6,14},{8,0},{10,2},{12,4},{14,6},{16,24},{18,... | collective-permute-start | bytes 49160 | tf_op jit(solution)/shard_map/ppermute | solution.py:56
  27.0 4.8 %collective-permute-start.7 = (f32[32,128]{1,0:T(8,128)S(1)}, f32[32,128]{1,0:T(8,128)S(1)}, u32[]{:S(2)}, u32[]{:S(2)}) collective-permute-start(f32[32,128]{1,0:T(8,128)S(1)} %add.32), channel_id=1, source_target_pairs={{0,16},{2,18},{4,20},{6,22},{8,24},{10,26},{12,28},{14,30},{16,0},... | collective-permute-start | bytes 49160 | tf_op jit(solution)/shard_map/ppermute | solution.py:56
  30.1 8.1 %collective-permute-start.10 = (f32[8,8192]{1,0:T(8,128)S(1)}, f32[8,8192]{1,0:T(8,128)S(1)}, u32[]{:S(2)}, u32[]{:S(2)}) collective-permute-start(f32[8,8192]{1,0:T(8,128)S(1)} %get-tuple-element.23), channel_id=1, source_target_pairs={{0,1},{1,0},{2,3},{3,2},{4,5},{5,4},{6,7},{7,6},{8,9},{9,8},{10,11... | collective-permute-start | bytes 786440 | tf_op jit(solution)/shard_map/ppermute | solution.py:30
  31.8 8.3 %collective-permute-start.12 = (f32[8,8192]{1,0:T(8,128)S(1)}, f32[8,8192]{1,0:T(8,128)S(1)}, u32[]{:S(2)}, u32[]{:S(2)}) collective-permute-start(f32[8,8192]{1,0:T(8,128)S(1)} %sum.1), channel_id=1, source_target_pairs={{4,0},{6,2},{8,4},{10,6},{12,8},{14,10},{16,12},{18,14},{20,16},{2... | collective-permute-start | bytes 786440 | tf_op jit(solution)/shard_map/ppermute | solution.py:26
  33.1 1.2 %collective-permute-start.8 = (f32[32,128]{1,0:T(8,128)S(1)}, f32[32,128]{1,0:T(8,128)S(1)}, u32[]{:S(2)}, u32[]{:S(2)}) collective-permute-start(f32[32,128]{1,0:T(8,128)S(1)} %add.33.ready), channel_id=1, source_target_pairs={{0,2},{2,0},{4,6},{6,4},{8,10},{10,8},{12,14},{14,12},{16,18},{18,... | collective-permute-start | bytes 49160 | tf_op jit(solution)/shard_map/ppermute | solution.py:56
  34.4 3.7 %collective-permute-start.9 = (f32[32,128]{1,0:T(8,128)S(1)}, f32[32,128]{1,0:T(8,128)S(1)}, u32[]{:S(2)}, u32[]{:S(2)}) collective-permute-start(f32[32,128]{1,0:T(8,128)S(1)} %add.34), channel_id=1, source_target_pairs={{0,1},{1,0},{2,3},{3,2},{4,5},{5,4},{6,7},{7,6},{8,9},{9,8},{10,11... | collective-permute-start | bytes 49160 | tf_op jit(solution)/shard_map/ppermute | solution.py:56

commit v3 on v1

--- a/solution.py
+++ b/solution.py
@@ -329,7 +329,7 @@
         1,
         [pltpu.SemaphoreType.DMA],
         51,
-        20_000_000_000,
+        2000000000,
     )
     if pair:
         other = swap_sub(vectors)
@@ -346,6 +346,7 @@
         (table, whole, levels, tiles),
         2,
         [pltpu.VMEM((BW + 1, width, rows_dev), F32)],
+        flops=20000000000,
     )
     if pair:
         whole2, across = call(
@@ -356,7 +357,7 @@
             [VMEM] * 2,
             (below, swap_sub(below), whole),
             1,
-            flops=20_000_000_000,
+            flops=20000000000,
         )
     else:
         whole2 = shifted(whole, BW)

time: 41 us -> 41 us (level)
  other arithmetic: 0.03 us -> 0.69 us
    add x1, other arithmetic: 0.01 us -> 0.66 us  [on_device(): tile_rows + LIVE_UNIT * tile_count]
    ppermute x2, waiting for transfers between devices: 1.08 us -> 0.62 us  [shifted(): lax.ppermute(value, 'blk', [(source, source + steps) for source in range(...]
  transfers between devices with their start and end apart: 13 -> 13, of which waited for: 9 -> 8; matrix products, arithmetic and copies ran while one was open for 0% -> 2% of each run, Pallas kernels for 18% -> 18%
where the time goes in v3:
time: 41 us; the launch traced here: 40.9 us
  starting transfers between devices  18.4 us (45%)
  waiting for transfers between devices  13 us (32%)
  Pallas kernels  7.95 us (19%)
  between operations  0.82 us (2%)
  other arithmetic  0.69 us (2%)
    ppermute x5, starting transfers between devices, run_rounds(): total = total + lax.ppermute(value, axis, pairs)  8.82 us
    ppermute x5, waiting for transfers between devices, run_rounds(): total = total + lax.ppermute(value, axis, pairs)  8.77 us
    pallas_call x9, Pallas kernels, call(): pl.pallas_call(kernel, out_shape=out_shape, in_specs=in_specs, out_specs=...  7.95 us
    ppermute x4, starting transfers between devices, swap_sub(): return lax.ppermute(value, 'sub', [(0, 1), (1, 0)])  4.76 us
    ppermute x2, starting transfers between devices, shifted(): lax.ppermute(value, 'blk', [(source, source + steps) for source in range(...  4.68 us
    ppermute x4, waiting for transfers between devices, swap_sub(): return lax.ppermute(value, 'sub', [(0, 1), (1, 0)])  2.76 us
    ppermute x2, waiting for transfers between devices, swap_core(): lax.ppermute(value, 'blk', [(i, i ^ 1) for i in range(lax.axis_size('blk'...  0.88 us
  transfers between devices with their start and end apart: 13, of which 8 were waited for; matrix products, arithmetic and copies ran while one was open for 2% of the time, Pallas kernels for 18%

profile of v3, /device:TPU:0, one launch (start us, length us, event | category | flops | bytes accessed | tf_op | source)
XLA Modules:
  0.0 40.9 jit_solution(13635840987779923331)
XLA Ops:
  0.0 3.0 %collective-permute-start = (bf16[8,8192]{1,0:T(8,128)(2,1)}, bf16[8,8192]{1,0:T(8,128)(2,1)S(1)}, u32[]{:S(2)}, u32[]{:S(2)}) collective-permute-start(bf16[8,8192]{1,0:T(8,128)(2,1)} %mine.1), channel_id=1, source_target_pairs={{0,1},{1,0},{2,3},{3,2},{4,5},{5,4},{6,7},{7,6},{8,9},{9,8},{10,11... | collective-permute-start | bytes 393224 | tf_op jit(solution)/shard_map/ppermute | solution.py:30
  3.0 3.4 %collective-permute-start.1 = (bf16[8,8192]{1,0:T(8,128)(2,1)}, bf16[8,8192]{1,0:T(8,128)(2,1)S(1)}, u32[]{:S(2)}, u32[]{:S(2)}) collective-permute-start(bf16[8,8192]{1,0:T(8,128)(2,1)} %mine.1), channel_id=1, source_target_pairs={{0,4},{2,6},{4,8},{6,10},{8,12},{10,14},{12,16},{14,18},{16,20},{1... | collective-permute-start | bytes 393224 | tf_op jit(solution)/shard_map/ppermute | solution.py:26
  7.0 0.7 %broadcast_add_fusion = s32[1,64]{1,0:T(1,128)S(1)} fusion(s32[1,64]{1,0:T(1,128)} %param.10, s32[]{:T(128)} %bitcast), kind=kLoop, calls=%fused_computation.1 | loop fusion | flops 64 | bytes 516 | tf_op jit(solution)/shard_map/add | solution.py:320
  7.7 1.6 %load.1.tiles = bf16[64,128,128]{2,1,0:T(8,128)(2,1)S(1)} custom-call(bf16[64,128,128]{2,1,0:T(8,128)(2,1)} %bitcast.5), custom_call_target="tpu_custom_call" | custom-call | flops 2000000000 | bytes 3000000 | tf_op jit(solution)/shard_map/load/pallas_call | solution.py:292
  9.4 0.6 %collective-permute-start.2 = (bf16[8,8192]{1,0:T(8,128)(2,1)S(1)}, bf16[8,8192]{1,0:T(8,128)(2,1)S(1)}, u32[]{:S(2)}, u32[]{:S(2)}) collective-permute-start(bf16[8,8192]{1,0:T(8,128)(2,1)S(1)} %collective-permute-done.1.own), channel_id=1, source_target_pairs={{0,1},{1,0},{2,3},{3,2},{4,5},{5,4},{6,7},{7,6},{8,9},{9,8},{10,11... | collective-permute-start | bytes 393224 | tf_op jit(solution)/shard_map/ppermute | solution.py:30
  10.0 1.7 %mirror.1 = (f32[16,8192]{1,0:T(8,128)S(1)}, f32[16,8192]{1,0:T(8,128)S(1)}, f32[16,8192]{1,0:T(8,128)S(1)}, f32[32,128]{1,0:T(8,128)S(1)}) custom-call(s32[3,64]{1,0:T(4,128)S(1)} %pad_add_fusion.table, bf16[16,8192]{1,0:T(8,128)(2,1)S(1)} %join.1.whole.vec, f32[64,128]{1,0:T(8,128)S(1)} %bitcast.3, bf16[64,128,128]{2,1,0:T(8,128)(2,1)S(1)} %load.1.tiles), custom_call_target="tpu_custom_call" | custom-call | flops 20000000000 | bytes 6000000 | tf_op jit(solution)/shard_map/mirror/pallas_call | solution.py:292
  11.7 2.7 %collective-permute-done.2.other = bf16[8,8192]{1,0:T(8,128)(2,1)S(1)} collective-permute-done((bf16[8,8192]{1,0:T(8,128)(2,1)S(1)}, bf16[8,8192]{1,0:T(8,128)(2,1)S(1)}, u32[]{:S(2)}, u32[]{:S(2)}) %collective-permute-start.2) | collective-permute-done | bytes 131104 | tf_op jit(solution)/shard_map/ppermute | solution.py:30
  14.7 0.6 %collective-permute-start.11 = (f32[8,8192]{1,0:T(8,128)S(1)}, f32[8,8192]{1,0:T(8,128)S(1)}, u32[]{:S(2)}, u32[]{:S(2)}) collective-permute-start(f32[8,8192]{1,0:T(8,128)S(1)} %get-tuple-element.26), channel_id=1, source_target_pairs={{0,1},{1,0},{2,3},{3,2},{4,5},{5,4},{6,7},{7,6},{8,9},{9,8},{10,11... | collective-permute-start | bytes 786440 | tf_op jit(solution)/shard_map/ppermute | solution.py:30
  15.3 0.9 %collective-permute-done.3.vec1 = bf16[16,8192]{1,0:T(8,128)(2,1)S(1)} collective-permute-done((bf16[16,8192]{1,0:T(8,128)(2,1)S(1)}, bf16[16,8192]{1,0:T(8,128)(2,1)S(1)}, u32[]{:S(2)}, u32[]{:S(2)}) %collective-permute-start.3) | collective-permute-done | bytes 262176 | tf_op jit(solution)/shard_map/ppermute | solution.py:34
  16.1 2.4 %direct.1 = (f32[8,8192]{1,0:T(8,128)S(1)}, f32[8,8192]{1,0:T(8,128)S(1)}, f32[32,128]{1,0:T(8,128)S(1)}) custom-call(s32[3,64]{1,0:T(4,128)S(1)} %pad_add_fusion.table, bf16[16,8192]{1,0:T(8,128)(2,1)S(1)} %join.1.whole.vec, bf16[16,8192]{1,0:T(8,128)(2,1)S(1)} %collective-permute-done.3.vec1, bf16[16,8192]{1,0:T(8,128)(2,1)S(1)} %get-tuple-element.17.vec2, ...), custom_call_target="tpu_custom_call" | custom-call | bytes 9000000 | tf_op jit(solution)/shard_map/direct/pallas_call | solution.py:292
  18.5 2.1 %collective-permute-start.5 = (f32[32,128]{1,0:T(8,128)S(1)}, f32[32,128]{1,0:T(8,128)S(1)}, u32[]{:S(2)}, u32[]{:S(2)}) collective-permute-start(f32[32,128]{1,0:T(8,128)S(1)} %get-tuple-element.21), channel_id=1, source_target_pairs={{0,4},{2,6},{4,0},{6,2},{8,12},{10,14},{12,8},{14,10},{16,20},{18,... | collective-permute-start | bytes 49160 | tf_op jit(solution)/shard_map/ppermute | solution.py:56
  20.6 1.7 %collective-permute-done.5 = f32[32,128]{1,0:T(8,128)S(1)} collective-permute-done((f32[32,128]{1,0:T(8,128)S(1)}, f32[32,128]{1,0:T(8,128)S(1)}, u32[]{:S(2)}, u32[]{:S(2)}) %collective-permute-start.5) | collective-permute-done | bytes 16416 | tf_op jit(solution)/shard_map/ppermute | solution.py:56
  22.3 3.0 %collective-permute-start.6 = (f32[32,128]{1,0:T(8,128)S(1)}, f32[32,128]{1,0:T(8,128)S(1)}, u32[]{:S(2)}, u32[]{:S(2)}) collective-permute-start(f32[32,128]{1,0:T(8,128)S(1)} %add.28), channel_id=1, source_target_pairs={{0,8},{2,10},{4,12},{6,14},{8,0},{10,2},{12,4},{14,6},{16,24},{18,... | collective-permute-start | bytes 49160 | tf_op jit(solution)/shard_map/ppermute | solution.py:56
  25.3 1.7 %collective-permute-done.6 = f32[32,128]{1,0:T(8,128)S(1)} collective-permute-done((f32[32,128]{1,0:T(8,128)S(1)}, f32[32,128]{1,0:T(8,128)S(1)}, u32[]{:S(2)}, u32[]{:S(2)}) %collective-permute-start.6) | collective-permute-done | bytes 16416 | tf_op jit(solution)/shard_map/ppermute | solution.py:56
  27.1 3.0 %collective-permute-start.7 = (f32[32,128]{1,0:T(8,128)S(1)}, f32[32,128]{1,0:T(8,128)S(1)}, u32[]{:S(2)}, u32[]{:S(2)}) collective-permute-start(f32[32,128]{1,0:T(8,128)S(1)} %add.29), channel_id=1, source_target_pairs={{0,16},{2,18},{4,20},{6,22},{8,24},{10,26},{12,28},{14,30},{16,0},... | collective-permute-start | bytes 49160 | tf_op jit(solution)/shard_map/ppermute | solution.py:56
  30.1 0.7 %collective-permute-start.10 = (f32[8,8192]{1,0:T(8,128)S(1)}, f32[8,8192]{1,0:T(8,128)S(1)}, u32[]{:S(2)}, u32[]{:S(2)}) collective-permute-start(f32[8,8192]{1,0:T(8,128)S(1)} %get-tuple-element.23), channel_id=1, source_target_pairs={{0,1},{1,0},{2,3},{3,2},{4,5},{5,4},{6,7},{7,6},{8,9},{9,8},{10,11... | collective-permute-start | bytes 786440 | tf_op jit(solution)/shard_map/ppermute | solution.py:30
  30.7 1.1 %collective-permute-done.7 = f32[32,128]{1,0:T(8,128)S(1)} collective-permute-done((f32[32,128]{1,0:T(8,128)S(1)}, f32[32,128]{1,0:T(8,128)S(1)}, u32[]{:S(2)}, u32[]{:S(2)}) %collective-permute-start.7) | collective-permute-done | bytes 16416 | tf_op jit(solution)/shard_map/ppermute | solution.py:56
  31.9 1.3 %collective-permute-start.12 = (f32[8,8192]{1,0:T(8,128)S(1)}, f32[8,8192]{1,0:T(8,128)S(1)}, u32[]{:S(2)}, u32[]{:S(2)}) collective-permute-start(f32[8,8192]{1,0:T(8,128)S(1)} %sum.1), channel_id=1, source_target_pairs={{4,0},{6,2},{8,4},{10,6},{12,8},{14,10},{16,12},{18,14},{20,16},{2... | collective-permute-start | bytes 786440 | tf_op jit(solution)/shard_map/ppermute | solution.py:26
  33.2 1.2 %collective-permute-done.8 = f32[32,128]{1,0:T(8,128)S(1)} collective-permute-done((f32[32,128]{1,0:T(8,128)S(1)}, f32[32,128]{1,0:T(8,128)S(1)}, u32[]{:S(2)}, u32[]{:S(2)}) %collective-permute-start.8) | collective-permute-done | bytes 16416 | tf_op jit(solution)/shard_map/ppermute | solution.py:56
  34.4 0.7 %collective-permute-start.9 = (f32[32,128]{1,0:T(8,128)S(1)}, f32[32,128]{1,0:T(8,128)S(1)}, u32[]{:S(2)}, u32[]{:S(2)}) collective-permute-start(f32[32,128]{1,0:T(8,128)S(1)} %add.31), channel_id=1, source_target_pairs={{0,1},{1,0},{2,3},{3,2},{4,5},{5,4},{6,7},{7,6},{8,9},{9,8},{10,11... | collective-permute-start | bytes 49160 | tf_op jit(solution)/shard_map/ppermute | solution.py:56
  35.1 3.1 %collective-permute-done.9 = f32[32,128]{1,0:T(8,128)S(1)} collective-permute-done((f32[32,128]{1,0:T(8,128)S(1)}, f32[32,128]{1,0:T(8,128)S(1)}, u32[]{:S(2)}, u32[]{:S(2)}) %collective-permute-start.9) | collective-permute-done | bytes 16416 | tf_op jit(solution)/shard_map/ppermute | solution.py:56
  38.2 1.3 %model.1.first = f32[8,8192]{1,0:T(8,128)S(1)} custom-call(f32[32,128]{1,0:T(8,128)S(1)} %add.32.small, bf16[16,8192]{1,0:T(8,128)(2,1)S(1)} %join.1.whole.vec, bf16[8,8192]{1,0:T(8,128)(2,1)S(1)} %copy-done, f32[64,128]{1,0:T(8,128)S(1)} %bitcast.4, f32[8,8192]{1,0:T(8,128)S(1)} %get-tuple-element.22.rest_0_, f32[8,8192]{1,0:T(8,128)S(1)} %collective-permute-done.10.rest_1_), custom_call_target="tpu_custom_call" | custom-call | bytes 6000000 | tf_op jit(solution)/shard_map/model/pallas_call | solution.py:292
  39.5 0.6 %collective-permute-done.12.second = f32[8,8192]{1,0:T(8,128)S(1)} collective-permute-done((f32[8,8192]{1,0:T(8,128)S(1)}, f32[8,8192]{1,0:T(8,128)S(1)}, u32[]{:S(2)}, u32[]{:S(2)}) %collective-permute-start.12) | collective-permute-done | bytes 262176 | tf_op jit(solution)/shard_map/ppermute | solution.py:26
  40.1 0.7 %last.1 = f32[8,8192]{1,0:T(8,128)} custom-call(f32[8,8192]{1,0:T(8,128)S(1)} %model.1.first, f32[8,8192]{1,0:T(8,128)S(1)} %collective-permute-done.12.second), custom_call_target="tpu_custom_call" | custom-call | bytes 3000000 | tf_op jit(solution)/shard_map/last/pallas_call | solution.py:292
  (26 shorter events, 0.4 us)
Async XLA Ops:
  0.0 9.4 %collective-permute-start = (bf16[8,8192]{1,0:T(8,128)(2,1)}, bf16[8,8192]{1,0:T(8,128)(2,1)S(1)}, u32[]{:S(2)}, u32[]{:S(2)}) collective-permute-start(bf16[8,8192]{1,0:T(8,128)(2,1)} %mine.1), channel_id=1, source_target_pairs={{0,1},{1,0},{2,3},{3,2},{4,5},{5,4},{6,7},{7,6},{8,9},{9,8},{10,11... | collective-permute-start | bytes 393224 | tf_op jit(solution)/shard_map/ppermute | solution.py:30
  3.0 6.5 %collective-permute-start.1 = (bf16[8,8192]{1,0:T(8,128)(2,1)}, bf16[8,8192]{1,0:T(8,128)(2,1)S(1)}, u32[]{:S(2)}, u32[]{:S(2)}) collective-permute-start(bf16[8,8192]{1,0:T(8,128)(2,1)} %mine.1), channel_id=1, source_target_pairs={{0,4},{2,6},{4,8},{6,10},{8,12},{10,14},{12,16},{14,18},{16,20},{1... | collective-permute-start | bytes 393224 | tf_op jit(solution)/shard_map/ppermute | solution.py:26
  7.7 1.7 %copy-start.2 = (s32[1,64]{1,0:T(1,128)S(1)}, s32[1,64]{1,0:T(1,128)}, u32[]{:S(2)}) copy-start(s32[1,64]{1,0:T(1,128)} %param.12) | copy-start | bytes 772
  7.7 1.7 %copy-start.3 = (s32[1,64]{1,0:T(1,128)S(1)}, s32[1,64]{1,0:T(1,128)}, u32[]{:S(2)}) copy-start(s32[1,64]{1,0:T(1,128)} %param.11) | copy-start | bytes 772
  7.7 1.7 %copy-start = (bf16[8,8192]{1,0:T(8,128)(2,1)S(1)}, bf16[8,8192]{1,0:T(8,128)(2,1)}, u32[]{:S(2)}) copy-start(bf16[8,8192]{1,0:T(8,128)(2,1)} %mine.1) | copy-start | bytes 393220
  7.7 2.3 %copy-start.1 = (f32[8192]{0:T(1024)S(1)}, f32[8192]{0:T(1024)}, u32[]{:S(2)}) copy-start(f32[8192]{0:T(1024)} %param.8) | copy-start | bytes 98308
  9.4 5.0 %collective-permute-start.2 = (bf16[8,8192]{1,0:T(8,128)(2,1)S(1)}, bf16[8,8192]{1,0:T(8,128)(2,1)S(1)}, u32[]{:S(2)}, u32[]{:S(2)}) collective-permute-start(bf16[8,8192]{1,0:T(8,128)(2,1)S(1)} %collective-permute-done.1.own), channel_id=1, source_target_pairs={{0,1},{1,0},{2,3},{3,2},{4,5},{5,4},{6,7},{7,6},{8,9},{9,8},{10,11... | collective-permute-start | bytes 393224 | tf_op jit(solution)/shard_map/ppermute | solution.py:30
  11.7 2.9 %collective-permute-start.4 = (f32[16,8192]{1,0:T(8,128)S(1)}, f32[16,8192]{1,0:T(8,128)S(1)}, u32[]{:S(2)}, u32[]{:S(2)}) collective-permute-start(f32[16,8192]{1,0:T(8,128)S(1)} %get-tuple-element.19), channel_id=1, source_target_pairs={{0,2},{2,0},{4,6},{6,4},{8,10},{10,8},{12,14},{14,12},{16,18},{18,... | collective-permute-start | bytes 1572872 | tf_op jit(solution)/shard_map/ppermute | solution.py:34
  14.5 1.6 %collective-permute-start.3 = (bf16[16,8192]{1,0:T(8,128)(2,1)S(1)}, bf16[16,8192]{1,0:T(8,128)(2,1)S(1)}, u32[]{:S(2)}, u32[]{:S(2)}) collective-permute-start(bf16[16,8192]{1,0:T(8,128)(2,1)S(1)} %get-tuple-element.16), channel_id=1, source_target_pairs={{0,2},{2,0},{4,6},{6,4},{8,10},{10,8},{12,14},{14,12},{16,18},{18,... | collective-permute-start | bytes 786440 | tf_op jit(solution)/shard_map/ppermute | solution.py:34
  14.7 17.1 %collective-permute-start.11 = (f32[8,8192]{1,0:T(8,128)S(1)}, f32[8,8192]{1,0:T(8,128)S(1)}, u32[]{:S(2)}, u32[]{:S(2)}) collective-permute-start(f32[8,8192]{1,0:T(8,128)S(1)} %get-tuple-element.26), channel_id=1, source_target_pairs={{0,1},{1,0},{2,3},{3,2},{4,5},{5,4},{6,7},{7,6},{8,9},{9,8},{10,11... | collective-permute-start | bytes 786440 | tf_op jit(solution)/shard_map/ppermute | solution.py:30
  18.5 3.8 %collective-permute-start.5 = (f32[32,128]{1,0:T(8,128)S(1)}, f32[32,128]{1,0:T(8,128)S(1)}, u32[]{:S(2)}, u32[]{:S(2)}) collective-permute-start(f32[32,128]{1,0:T(8,128)S(1)} %get-tuple-element.21), channel_id=1, source_target_pairs={{0,4},{2,6},{4,0},{6,2},{8,12},{10,14},{12,8},{14,10},{16,20},{18,... | collective-permute-start | bytes 49160 | tf_op jit(solution)/shard_map/ppermute | solution.py:56
  22.3 4.7 %collective-permute-start.6 = (f32[32,128]{1,0:T(8,128)S(1)}, f32[32,128]{1,0:T(8,128)S(1)}, u32[]{:S(2)}, u32[]{:S(2)}) collective-permute-start(f32[32,128]{1,0:T(8,128)S(1)} %add.28), channel_id=1, source_target_pairs={{0,8},{2,10},{4,12},{6,14},{8,0},{10,2},{12,4},{14,6},{16,24},{18,... | collective-permute-start | bytes 49160 | tf_op jit(solution)/shard_map/ppermute | solution.py:56
  27.1 4.8 %collective-permute-start.7 = (f32[32,128]{1,0:T(8,128)S(1)}, f32[32,128]{1,0:T(8,128)S(1)}, u32[]{:S(2)}, u32[]{:S(2)}) collective-permute-start(f32[32,128]{1,0:T(8,128)S(1)} %add.29), channel_id=1, source_target_pairs={{0,16},{2,18},{4,20},{6,22},{8,24},{10,26},{12,28},{14,30},{16,0},... | collective-permute-start | bytes 49160 | tf_op jit(solution)/shard_map/ppermute | solution.py:56
  30.1 8.1 %collective-permute-start.10 = (f32[8,8192]{1,0:T(8,128)S(1)}, f32[8,8192]{1,0:T(8,128)S(1)}, u32[]{:S(2)}, u32[]{:S(2)}) collective-permute-start(f32[8,8192]{1,0:T(8,128)S(1)} %get-tuple-element.23), channel_id=1, source_target_pairs={{0,1},{1,0},{2,3},{3,2},{4,5},{5,4},{6,7},{7,6},{8,9},{9,8},{10,11... | collective-permute-start | bytes 786440 | tf_op jit(solution)/shard_map/ppermute | solution.py:30
  31.9 8.3 %collective-permute-start.12 = (f32[8,8192]{1,0:T(8,128)S(1)}, f32[8,8192]{1,0:T(8,128)S(1)}, u32[]{:S(2)}, u32[]{:S(2)}) collective-permute-start(f32[8,8192]{1,0:T(8,128)S(1)} %sum.1), channel_id=1, source_target_pairs={{4,0},{6,2},{8,4},{10,6},{12,8},{14,10},{16,12},{18,14},{20,16},{2... | collective-permute-start | bytes 786440 | tf_op jit(solution)/shard_map/ppermute | solution.py:26
  33.2 1.2 %collective-permute-start.8 = (f32[32,128]{1,0:T(8,128)S(1)}, f32[32,128]{1,0:T(8,128)S(1)}, u32[]{:S(2)}, u32[]{:S(2)}) collective-permute-start(f32[32,128]{1,0:T(8,128)S(1)} %add.30.ready), channel_id=1, source_target_pairs={{0,2},{2,0},{4,6},{6,4},{8,10},{10,8},{12,14},{14,12},{16,18},{18,... | collective-permute-start | bytes 49160 | tf_op jit(solution)/shard_map/ppermute | solution.py:56
  34.4 3.7 %collective-permute-start.9 = (f32[32,128]{1,0:T(8,128)S(1)}, f32[32,128]{1,0:T(8,128)S(1)}, u32[]{:S(2)}, u32[]{:S(2)}) collective-permute-start(f32[32,128]{1,0:T(8,128)S(1)} %add.31), channel_id=1, source_target_pairs={{0,1},{1,0},{2,3},{3,2},{4,5},{5,4},{6,7},{7,6},{8,9},{9,8},{10,11... | collective-permute-start | bytes 49160 | tf_op jit(solution)/shard_map/ppermute | solution.py:56
